TPU v7x, 256 devices: a whole 4x4x8 slice. The times are simulated.
256 devices in a mesh: ty: 16 (over y_hi, x, core), tx: 16 (over z, y_lo).
Axes of the slice: x: 4, y: 4 (y_hi: 2, y_lo: 2; y = y_hi * 2 + y_lo), z: 8, core: 2. Of those that a mesh axis runs over, the one named last changes fastest.
Arguments:
- object_field: float32 [2, 4096, 4096], P(None, 'ty', 'tx'), may hold values from -6 to 6
- probe_modes: float32 [2, 2, 256, 256], replicated, may hold values from -6 to 6
- intensities: float32 [16, 16, 3, 256, 256], P('ty', 'tx'), may hold values from 0.25 to 16
- offsets: int32 [16, 16, 3, 2], P('ty', 'tx'), may hold values from 0 to 256
- counts: int32 [16, 16], replicated, may hold values from 1 to 3, as said below
Outputs:
- object_grad: float32 [2, 4096, 4096], P(None, 'ty', 'tx')
- probe_grad: float32 [2, 2, 256, 256], replicated
Inputs may be any that keep to these rules, and one draw needn't show every extreme that they name: Tile (a, b) uses slots 0 to counts[a, b] - 1 of intensities and offsets; its other slots are ignored. In every draw some tile uses all 3 slots.
All inputs are finite; a program needn't handle non-finite values.
Results may differ from a plain program's by a relative error of at most 0.0003.
Values sent between devices are 32-bit elements; how exact they have to be, the bound alone decides.
A program may use at most 64 MiB of HBM per device.

v0:
```python
import math

import jax
import jax.numpy as jnp
from jax import lax
from jax.sharding import PartitionSpec as P

FLOOR = 0.5
exact_mode = lax.Precision.HIGHEST


def shifted(value, axis, steps):
    count = lax.axis_size(axis)
    initial, last = (max(0, -steps), min(count, count - steps))
    return lax.ppermute(value, axis, [(source, source + steps) for source in range(initial, last)])


def padded_2(shard, sides, width):
    for axis, dim in sides:
        count, length = (lax.axis_size(axis), shard.shape[dim])
        up = [(i, (i + 1) % count) for i in range(count - 1)]
        down = [(j, i) for i, j in up]
        last = lax.slice_in_dim(shard, length - width, length, axis=dim)
        initial = lax.slice_in_dim(shard, 0, width, axis=dim)
        before = lax.ppermute(last, axis, up)
        after = lax.ppermute(initial, axis, down)
        shard = jnp.concatenate([before, shard, after], axis=dim)
    return shard


def fourier_tables(pattern):
    steps_range = jnp.arange(pattern, dtype=jnp.int32)
    product = steps_range[:, None] * steps_range[None, :] % pattern
    angle = 2.0 * math.pi / pattern * product.astype(jnp.float32)
    norm_factor = 1.0 / math.sqrt(pattern)
    return (jnp.cos(angle) * norm_factor, jnp.sin(angle) * norm_factor)


def transform(real_part, imag_part, cosine, sine, direction):
    left_real = jnp.einsum(
        "kn,mnj->mkj", cosine, real_part, precision=exact_mode
    ) - direction * jnp.einsum("kn,mnj->mkj", sine, imag_part, precision=exact_mode)
    left_imag = jnp.einsum(
        "kn,mnj->mkj", cosine, imag_part, precision=exact_mode
    ) + direction * jnp.einsum("kn,mnj->mkj", sine, real_part, precision=exact_mode)
    out_real = jnp.einsum(
        "mkn,nj->mkj", left_real, cosine, precision=exact_mode
    ) - direction * jnp.einsum("mkn,nj->mkj", left_imag, sine, precision=exact_mode)
    out_imag = jnp.einsum(
        "mkn,nj->mkj", left_imag, cosine, precision=exact_mode
    ) + direction * jnp.einsum("mkn,nj->mkj", left_real, sine, precision=exact_mode)
    return (out_real, out_imag)


def slot_gradient(patch, measured, probe_modes, cosine, sine):
    probe_real, probe_imag = (probe_modes[0], probe_modes[1])
    patch_real, patch_imag = (patch[0], patch[1])
    wave_real = probe_real * patch_real - probe_imag * patch_imag
    wave_imag = probe_real * patch_imag + probe_imag * patch_real
    far_real, far_imag = transform(wave_real, wave_imag, cosine, sine, -1.0)
    amplitude = jnp.sqrt(jnp.sum(far_real * far_real + far_imag * far_imag, axis=0))
    factor = 1.0 - jnp.sqrt(measured) / jnp.maximum(amplitude, FLOOR)
    back_real, back_imag = transform(far_real * factor, far_imag * factor, cosine, sine, 1.0)
    object_part = jnp.stack(
        [
            jnp.sum(probe_real * back_real + probe_imag * back_imag, axis=0),
            jnp.sum(probe_real * back_imag - probe_imag * back_real, axis=0),
        ]
    )
    probe_part = jnp.stack(
        [
            patch_real * back_real + patch_imag * back_imag,
            patch_real * back_imag - patch_imag * back_real,
        ]
    )
    return (object_part, probe_part)


def pass_columns(piece, offset):
    return shifted(piece, "tx", offset)


def pass_rows(piece, offset):
    return shifted(piece, "ty", offset)


def shards(object_field, probe_modes, intensities, offsets, counts):
    tile_cells = object_field.shape[1]
    pattern = probe_modes.shape[2]
    margin = pattern // 2
    cosine, sine = fourier_tables(pattern)
    padded = padded_2(object_field, (("ty", 1), ("tx", 2)), margin)
    tile_row = lax.axis_index("ty")
    tile_col = lax.axis_index("tx")
    listed = counts[tile_row, tile_col]
    measured_all = intensities[0, 0]
    spots = offsets[0, 0]

    def window(field, slot_index):
        return lax.dynamic_slice(
            field, (0, spots[slot_index, 0], spots[slot_index, 1]), (2, pattern, pattern)
        )

    def add_patch(grid, part, slot_index):
        start = (0, spots[slot_index, 0], spots[slot_index, 1])
        current = lax.dynamic_slice(grid, start, part.shape)
        return lax.dynamic_update_slice(grid, current + part, start)

    def home_step(slot_index, carry):
        grid, probe_sum = carry
        object_part, probe_part = slot_gradient(
            window(padded, slot_index), measured_all[slot_index], probe_modes, cosine, sine
        )
        return (add_patch(grid, object_part, slot_index), probe_sum + probe_part)

    start_carry = (jnp.zeros(padded.shape, jnp.float32), jnp.zeros(probe_modes.shape, jnp.float32))
    grid, probe_sum = lax.fori_loop(0, listed, home_step, start_carry)
    from_right = pass_columns(grid[:, :, :margin], -1)
    from_left = pass_columns(grid[:, :, tile_cells + margin :], 1)
    middle = grid[:, :, margin : tile_cells + margin]
    middle = middle.at[:, :, tile_cells - margin :].add(from_right)
    middle = middle.at[:, :, :margin].add(from_left)
    from_below = pass_rows(middle[:, :margin, :], -1)
    from_above = pass_rows(middle[:, tile_cells + margin :, :], 1)
    inner = middle[:, margin : tile_cells + margin, :]
    inner = inner.at[:, tile_cells - margin :, :].add(from_below)
    inner = inner.at[:, :margin, :].add(from_above)
    probe_total = lax.psum(probe_sum, ("ty", "tx"))
    return (inner, probe_total / (lax.axis_size("ty") * lax.axis_size("tx")))


def solution(mesh):
    placed = (
        P(None, "ty", "tx"),
        P(),
        P("ty", "tx", None, None, None),
        P("ty", "tx", None, None),
        P(),
    )
    return jax.shard_map(
        shards, mesh=mesh, in_specs=placed, out_specs=(P(None, "ty", "tx"), P()), check_vma=False
    )
```

profile of v0, /device:TPU:1, one launch (start us, length us, event | category | flops | bytes accessed | tf_op | source)
XLA Modules:
  0.0 472.0 jit_solution(17021481430789335461)
XLA Ops:
  7.2 0.0 all-reduce.2.cloned.1.call-start
  7.2 1.1 fusion.148
  8.3 4.5 collective-permute-start
  12.8 1.9 collective-permute-start.1
  14.7 1.4 collective-permute-done
  16.1 1.1 constant_dynamic-update-slice_fusion.1
  17.2 3.3 collective-permute-done.1
  20.5 0.1 fusion.147
  20.6 3.2 collective-permute-start.2
  23.8 1.3 collective-permute-start.3
  25.1 1.3 dynamic_slice.20
  26.4 16.6 %collective-permute-done.2 = f32[2,512,128]{2,1,0:T(8,128)S(1)} collective-permute-done((f32[2,512,128]{2,1,0:T(8,128)S(1)}, f32[2,512,128]{2,1,0:T(8,128)S(1)}, u32[]{:S(2)}, u32[]{:S(2)}) %collective-permute-start.2) | collective-permute-done | bytes 524320 | tf_op jit(solution)/shard_map/ppermute | solution.py:25
  43.0 0.0 collective-permute-done.3
  43.0 1.5 pad_maximum_fusion
  44.5 0.0 copy-start.2
  44.5 0.1 broadcast_in_dim.5
  44.6 1.6 broadcast_in_dim.4
  46.2 0.0 copy-done.2
  46.2 0.0 copy-done.4
  46.2 46.2 %while.18 = (s32[]{:T(128)}, f32[2,512,512]{2,1,0:T(8,128)}, f32[2,2,256,256]{3,2,1,0:T(8,128)S(1)}, s32[]{:T(128)}, s32[3,2]{0,1:T(2,128)S(1)}, /*index=5*/f32[...) while((s32[]{:T(128)}, f32[2,512,512]{2,1,0:T(8,128)}, ...), condition=%wide.region_4.5_spmd.clone.clone, body=%wide.region_0.4_spmd.clone.clone.sunk | while | flops 6464995328 | bytes 37749028 | solution.py:117
  46.8 0.7 constant_dynamic-slice_fusion.3
  51.2 1.3 dynamic-slice_bitcast_fusion.3
  52.5 1.9 fusion.238
  54.4 1.9 fusion.239
  56.3 1.8 fusion.241
  58.2 1.9 fusion.235
  60.1 1.9 fusion.236
  62.0 1.8 fusion.237
  63.8 1.8 fusion.240
  65.6 1.8 add_reduce_fusion.2
  67.5 1.1 fusion.242
  68.6 1.8 fusion.246
  70.5 1.9 fusion.247
  72.3 1.8 fusion.243
  74.2 1.9 fusion.244
  76.0 1.8 fusion.245
  77.9 1.9 convolution_add_fusion.3
  79.7 1.8 fusion.248
  81.6 2.1 add_bitcast_fusion.2
  83.7 1.4 maximum_add_fusion.4
  85.0 0.3 maximum_add_fusion.5
  85.3 6.5 %dynamic_update_slice.6 = f32[2,512,512]{2,1,0:T(8,128)} dynamic-update-slice(f32[2,512,512]{2,1,0:T(8,128)} %get-tuple-element.328, f32[2,256,256]{2,1,0:T(8,128)S(1)} %maximum_add_fusion.4, s32[]{:T(128)} %constant.145.clone.1..sunk, s32[]{:T(128)S(6)} %select_n.174, s32[]{:T(128)S(6)} %select_n.175) | dynamic-update-slice | bytes 1048580 | tf_op jit(solution)/shard_map/while/body/dynamic_update_slice | solution.py:107
  92.4 0.0 copy-start
  92.4 0.0 copy-start.1
  92.4 1.5 slice.146
  93.9 1.3 collective-permute-start.4
  95.2 1.3 slice.144
  96.5 10.3 %collective-permute-done.4 = f32[2,512,128]{2,1,0:T(8,128)S(1)} collective-permute-done((f32[2,512,128]{2,1,0:T(8,128)S(1)}, f32[2,512,128]{2,1,0:T(8,128)S(1)}, u32[]{:S(2)}, u32[]{:S(2)}) %collective-permute-start.4) | collective-permute-done | bytes 524320 | tf_op jit(solution)/shard_map/ppermute | solution.py:15
  106.9 0.0 copy-done.1
  106.9 0.1 fusion.145
  107.0 0.0 copy-done
  107.0 2.3 collective-permute-start.5
  109.3 0.0 all-reduce.2.cloned.1.call-update
  109.3 6.1 %collective-permute-done.5 = f32[2,512,128]{2,1,0:T(8,128)S(1)} collective-permute-done((f32[2,512,128]{2,1,0:T(8,128)S(1)}, f32[2,512,128]{2,1,0:T(8,128)S(1)}, u32[]{:S(2)}, u32[]{:S(2)}) %collective-permute-start.5) | collective-permute-done | bytes 524320 | tf_op jit(solution)/shard_map/ppermute | solution.py:15
  115.3 0.1 fusion.142
  115.5 49.5 %collective-permute-start.7 = (f32[2,128,256]{2,1,0:T(8,128)S(1)}, f32[2,128,256]{2,1,0:T(8,128)S(1)}, u32[]{:S(2)}, u32[]{:S(2)}) collective-permute-start(f32[2,128,256]{2,1,0:T(8,128)S(1)} %get-tuple-element.238), channel_id=1, source_target_pairs={{0,16},{16,32},{32,48},{48,64},{64,80},{80,96},{96,112},{112,128},... | collective-permute-start | bytes 786440 | tf_op jit(solution)/shard_map/ppermute | solution.py:15
  165.0 1.9 collective-permute-start.6
  167.0 295.0 %all-reduce.2.cloned.1.call-done = f32[2,2,256,256]{3,2,1,0:T(8,128)} async-done(((f32[2,2,256,256]{3,2,1,0:T(8,128)}), f32[2,2,256,256]{3,2,1,0:T(8,128)}) %all-reduce.2.cloned.1.call-update) | async-done | bytes 1048592 | tf_op jit(solution)/shard_map/psum | solution.py:128
  461.9 2.3 broadcast_multiply_fusion
  464.3 0.0 collective-permute-done.6
  464.3 0.0 collective-permute-done.7
  464.3 0.1 fusion.143
  464.4 0.0 copy-start.3
  464.4 0.8 copy-done.3
  (6 shorter events, 0.1 us)
Async XLA Ops:
  7.2 454.8 %all-reduce.2.cloned.1.call-start = ((), (), s32[]{:S(2)}) async-start(), calls=%async_computation | async-start | bytes 2097152 | tf_op jit(solution)/shard_map/psum | solution.py:128
  8.3 7.8 %collective-permute-start = (f32[2,128,256]{2,1,0:T(8,128)S(1)}, f32[2,128,256]{2,1,0:T(8,128)S(1)}, u32[]{:S(2)}, u32[]{:S(2)}) collective-permute-start(f32[2,128,256]{2,1,0:T(8,128)S(1)} %get-tuple-element.243), channel_id=1, source_target_pairs={{0,16},{16,32},{32,48},{48,64},{64,80},{80,96},{96,112},{112,128},... | collective-permute-start | bytes 786440 | tf_op jit(solution)/shard_map/ppermute | solution.py:25
  12.8 7.7 %collective-permute-start.1 = (f32[2,128,256]{2,1,0:T(8,128)S(1)}, f32[2,128,256]{2,1,0:T(8,128)S(1)}, u32[]{:S(2)}, u32[]{:S(2)}) collective-permute-start(f32[2,128,256]{2,1,0:T(8,128)S(1)} %get-tuple-element.242), channel_id=1, source_target_pairs={{16,0},{32,16},{48,32},{64,48},{80,64},{96,80},{112,96},{128,112},... | collective-permute-start | bytes 786440 | tf_op jit(solution)/shard_map/ppermute | solution.py:26
  20.6 22.4 %collective-permute-start.2 = (f32[2,512,128]{2,1,0:T(8,128)S(1)}, f32[2,512,128]{2,1,0:T(8,128)S(1)}, u32[]{:S(2)}, u32[]{:S(2)}) collective-permute-start(f32[2,512,128]{2,1,0:T(8,128)S(1)} %get-tuple-element.240), channel_id=1, source_target_pairs={{0,1},{1,2},{2,3},{3,4},{4,5},{5,6},{6,7},{7,8},{8,9},{9,10},{10,1... | collective-permute-start | bytes 1572872 | tf_op jit(solution)/shard_map/ppermute | solution.py:25
  23.8 19.1 %collective-permute-start.3 = (f32[2,512,128]{2,1,0:T(8,128)S(1)}, f32[2,512,128]{2,1,0:T(8,128)S(1)}, u32[]{:S(2)}, u32[]{:S(2)}) collective-permute-start(f32[2,512,128]{2,1,0:T(8,128)S(1)} %get-tuple-element.241), channel_id=1, source_target_pairs={{1,0},{2,1},{3,2},{4,3},{5,4},{6,5},{7,6},{8,7},{9,8},{10,9},{11,1... | collective-permute-start | bytes 1572872 | tf_op jit(solution)/shard_map/ppermute | solution.py:26
  44.5 1.7 copy-start.2
  44.5 1.7 copy-start.4
  92.4 14.6 %copy-start = (f32[2,2,256,256]{3,2,1,0:T(8,128)}, f32[2,2,256,256]{3,2,1,0:T(8,128)S(1)}, u32[]{:S(2)}) copy-start(f32[2,2,256,256]{3,2,1,0:T(8,128)S(1)} %get-tuple-element.147) | copy-start | bytes 3145732
  92.4 14.5 %copy-start.1 = (f32[2,512,512]{2,1,0:T(8,128)S(1)}, f32[2,512,512]{2,1,0:T(8,128)}, u32[]{:S(2)}) copy-start(f32[2,512,512]{2,1,0:T(8,128)} %get-tuple-element.146) | copy-start | bytes 6291460
  93.9 12.9 %collective-permute-start.4 = (f32[2,512,128]{2,1,0:T(8,128)S(1)}, f32[2,512,128]{2,1,0:T(8,128)S(1)}, u32[]{:S(2)}, u32[]{:S(2)}) collective-permute-start(f32[2,512,128]{2,1,0:T(8,128)S(1)} %slice.146), channel_id=1, source_target_pairs={{1,0},{2,1},{3,2},{4,3},{5,4},{6,5},{7,6},{8,7},{9,8},{10,9},{11,1... | collective-permute-start | bytes 1572872 | tf_op jit(solution)/shard_map/ppermute | solution.py:15
  107.0 8.4 %collective-permute-start.5 = (f32[2,512,128]{2,1,0:T(8,128)S(1)}, f32[2,512,128]{2,1,0:T(8,128)S(1)}, u32[]{:S(2)}, u32[]{:S(2)}) collective-permute-start(f32[2,512,128]{2,1,0:T(8,128)S(1)} %get-tuple-element.236), channel_id=1, source_target_pairs={{0,1},{1,2},{2,3},{3,4},{4,5},{5,6},{6,7},{7,8},{8,9},{9,10},{10,1... | collective-permute-start | bytes 1572872 | tf_op jit(solution)/shard_map/ppermute | solution.py:15
  115.5 348.8 %collective-permute-start.7 = (f32[2,128,256]{2,1,0:T(8,128)S(1)}, f32[2,128,256]{2,1,0:T(8,128)S(1)}, u32[]{:S(2)}, u32[]{:S(2)}) collective-permute-start(f32[2,128,256]{2,1,0:T(8,128)S(1)} %get-tuple-element.238), channel_id=1, source_target_pairs={{0,16},{16,32},{32,48},{48,64},{64,80},{80,96},{96,112},{112,128},... | collective-permute-start | bytes 786440 | tf_op jit(solution)/shard_map/ppermute | solution.py:15
  165.0 299.2 %collective-permute-start.6 = (f32[2,128,256]{2,1,0:T(8,128)S(1)}, f32[2,128,256]{2,1,0:T(8,128)S(1)}, u32[]{:S(2)}, u32[]{:S(2)}) collective-permute-start(f32[2,128,256]{2,1,0:T(8,128)S(1)} %get-tuple-element.239), channel_id=1, source_target_pairs={{16,0},{32,16},{48,32},{64,48},{80,64},{96,80},{112,96},{128,112},... | collective-permute-start | bytes 786440 | tf_op jit(solution)/shard_map/ppermute | solution.py:15
  464.4 0.8 copy-start.3
Sparse Core Ops, SparseCore 0:
  109.4 352.4 all-reduce.1
where the time goes:
time: 472 us
  waiting for transfers between devices  333 us (71%)
  starting transfers between devices  66 us (14%)
  matrix products  29.9 us (6%)
  local copies, waits for them, and re-layouts  17.3 us (4%)
  between operations  14.2 us (3%)
  other arithmetic  6.86 us (1%)
  loops' own time  5.13 us (1%)
    psum x1, waiting for transfers between devices, shards(): probe_total = lax.psum(probe_sum, ('ty', 'tx'))  295 us
    ppermute x4, starting transfers between devices, shifted(): lax.ppermute(value, axis, [(source, source + steps) for source in range(i...  55 us
    ppermute x2, waiting for transfers between devices, padded_2(): before = lax.ppermute(last, axis, up)  17.9 us
    ppermute x4, waiting for transfers between devices, shifted(): lax.ppermute(value, axis, [(source, source + steps) for source in range(i...  16.4 us
  transfers between devices with their start and end apart: 9, of which 6 were waited for; matrix products, arithmetic and copies ran while one was open for 1% of the time, Pallas kernels for 0%

commit v1 on v0

v1 whole, which is shorter than its diff:
```python
import functools

import jax
import jax.numpy as jnp
import numpy as np
from jax import lax
from jax.experimental import pallas as pl
from jax.experimental.pallas import tpu as pltpu
from jax.sharding import PartitionSpec as P

FLOOR = 0.5
MESH = pl.DeviceIdType.MESH
F32 = jnp.float32
BF16 = jnp.bfloat16
VMEM = pl.BlockSpec(memory_space=pltpu.VMEM)
SMEM = pl.BlockSpec(memory_space=pltpu.SMEM)


def tables(pattern):
    half = pattern // 2
    n = np.arange(half)[:, None]
    out = []
    for parity in (0, 1):
        k = 2 * np.arange(half)[None, :] + parity
        angle = 2.0 * np.pi * ((n * k) % pattern) / pattern
        c, s = np.cos(angle) / np.sqrt(pattern), np.sin(angle) / np.sqrt(pattern)
        full = np.block([[c, -s], [s, c]])
        hi = full.astype(BF16)
        lo = (full - hi.astype(np.float64)).astype(BF16)
        out.append((hi, lo))
    (eh, el), (oh, ol) = out
    right = np.stack([np.concatenate([h, h, l], 0) for h, l in out])
    right_back = np.stack([np.concatenate([h.T, h.T, l.T], 0) for h, l in out])
    left = np.stack([np.concatenate([h.T, h.T, l.T], 1) for h, l in out])
    left_back = np.stack([np.concatenate([h, h, l], 1) for h, l in out])
    return right, left, left_back, right_back


def reorder_table(pattern):
    half = pattern // 2
    table = np.zeros((pattern, pattern), np.float32)
    table[2 * np.arange(half), np.arange(half)] = 1
    table[2 * np.arange(half) + 1, half + np.arange(half)] = 1
    return table.astype(BF16)


def split(a):
    hi = a.astype(BF16)
    return hi, (a - hi.astype(F32)).astype(BF16)


def times_right(a, table):
    hi, lo = split(a)
    return jnp.dot(jnp.concatenate([hi, lo, hi], axis=1), table, preferred_element_type=F32)


def times_left(table, a):
    hi, lo = split(a)
    return jnp.dot(table, jnp.concatenate([hi, lo, hi], axis=0), preferred_element_type=F32)


def slots_kernel(
    counts, spots, ext, probe, measured, right, left, left_back, right_back, order, order_t,
    grid, probe_sum, factor,
):
    pattern = probe.shape[2]
    half = pattern // 2
    modes = probe.shape[1]
    wide, tall = pattern + half, pattern + 8
    listed = counts[lax.axis_index("ty"), lax.axis_index("tx")]
    grid[...] = jnp.zeros(grid.shape, F32)
    probe_sum[...] = jnp.zeros(probe_sum.shape, F32)

    @pl.loop(0, listed)
    def _(slot):
        row = spots[slot, 0]
        col = spots[slot, 1]
        block = (col >= half).astype(jnp.int32)
        rest = col - block * half
        first = pl.multiple_of(block * half, half)
        group = jnp.minimum(lax.div(row, 8), pattern // 8 - 1)
        skip = row - group * 8
        top_row = pl.multiple_of(group * 8, 8)

        def window(part):
            strip = ext[part, pl.ds(top_row, tall), pl.ds(first, wide)]
            strip = pltpu.roll(strip, lax.rem(tall - skip, tall), 0)[:pattern]
            return pltpu.roll(strip, lax.rem(wide - rest, wide), 1)[:, :pattern]

        xr, xi = window(0), window(1)

        root = jnp.sqrt(measured[slot])
        hi, lo = split(root)
        root = jnp.dot(hi, order[...], preferred_element_type=F32) + jnp.dot(
            lo, order[...], preferred_element_type=F32
        )
        hi, lo = split(root)
        root = jnp.dot(order_t[...], hi, preferred_element_type=F32) + jnp.dot(
            order_t[...], lo, preferred_element_type=F32
        )

        far = []
        for m in range(modes):
            pr, pi = probe[0, m], probe[1, m]
            wr = pr * xr - pi * xi
            wi = pr * xi + pi * xr
            u = jnp.concatenate([wr[:, :half] + wr[:, half:], wi[:, :half] + wi[:, half:]], 1)
            v = jnp.concatenate([wr[:, :half] - wr[:, half:], wi[:, :half] - wi[:, half:]], 1)
            even = times_right(u, right[0])
            odd = times_right(v, right[1])
            us = jnp.concatenate([even[:half] + even[half:], odd[:half] + odd[half:]], 1)
            vs = jnp.concatenate([even[:half] - even[half:], odd[:half] - odd[half:]], 1)
            us, vs = regroup(us, half), regroup(vs, half)
            far.append((times_left(left[0], us), times_left(left[1], vs)))

        for parity in (0, 1):
            power = 0.0
            for m in range(modes):
                g = far[m][parity]
                power = power + g[:half] * g[:half] + g[half:] * g[half:]
            amplitude = jnp.maximum(jnp.sqrt(power), FLOOR)
            factor[parity] = 1.0 - root[parity * half : (parity + 1) * half] / amplitude

        object_r = 0.0
        object_i = 0.0
        for m in range(modes):
            pr, pi = probe[0, m], probe[1, m]
            halves = []
            for parity in (0, 1):
                f = factor[parity]
                g = far[m][parity]
                halves.append(times_left(left_back[parity], jnp.concatenate([g[:half] * f, g[half:] * f], 0)))
            top, bottom = halves[0] + halves[1], halves[0] - halves[1]
            k = []
            for parity in (0, 1):
                at = slice(parity * half, (parity + 1) * half)
                z = jnp.concatenate(
                    [
                        jnp.concatenate([top[:half, at], top[half:, at]], 1),
                        jnp.concatenate([bottom[:half, at], bottom[half:, at]], 1),
                    ],
                    0,
                )
                k.append(times_right(z, right_back[parity]))
            near, off = k[0] + k[1], k[0] - k[1]
            br = jnp.concatenate([near[:, :half], off[:, :half]], 1)
            bi = jnp.concatenate([near[:, half:], off[:, half:]], 1)
            object_r = object_r + pr * br + pi * bi
            object_i = object_i + pr * bi - pi * br
            probe_sum[0, m] += xr * br + xi * bi
            probe_sum[1, m] += xr * bi - xi * br

        for part, piece in ((0, object_r), (1, object_i)):
            padded = jnp.concatenate([piece, jnp.zeros((pattern, half), F32)], 1)
            padded = pltpu.roll(padded, rest, 1)
            padded = jnp.concatenate([padded, jnp.zeros((8, wide), F32)], 0)
            grid[part, pl.ds(top_row, tall), pl.ds(first, wide)] += pltpu.roll(padded, skip, 0)


def regroup(a, half):
    re = jnp.concatenate([a[:, :half], a[:, 2 * half : 3 * half]], 1)
    im = jnp.concatenate([a[:, half : 2 * half], a[:, 3 * half :]], 1)
    return jnp.concatenate([re, im], 0)


def slots(counts, spots, ext, probe, measured):
    pattern = probe.shape[2]
    right, left, left_back, right_back = tables(pattern)
    order = reorder_table(pattern)
    extent = ext.shape[1]
    return pl.pallas_call(
        slots_kernel,
        out_shape=(
            jax.ShapeDtypeStruct(ext.shape, F32),
            jax.ShapeDtypeStruct(probe.shape, F32),
        ),
        in_specs=[SMEM, SMEM] + [VMEM] * 9,
        out_specs=(VMEM, VMEM),
        scratch_shapes=[pltpu.VMEM((2, pattern // 2, pattern), F32)],
        name="slots",
    )(
        counts, spots, ext, probe, measured,
        jnp.asarray(right), jnp.asarray(left), jnp.asarray(left_back), jnp.asarray(right_back),
        jnp.asarray(order), jnp.asarray(order.T),
    )


def remote(src, dst, send, recv, ty, tx):
    return pltpu.make_async_remote_copy(
        src_ref=src, dst_ref=dst, send_sem=send, recv_sem=recv, device_id=(ty, tx), device_id_type=MESH
    )


def neighbours():
    ty, tx = lax.axis_index("ty"), lax.axis_index("tx")
    n, m = lax.axis_size("ty"), lax.axis_size("tx")
    up, down = lax.rem(ty + n - 1, n), lax.rem(ty + 1, n)
    west, east = lax.rem(tx + m - 1, m), lax.rem(tx + 1, m)
    return ty, tx, n, m, up, down, west, east


def greet(peers):
    barrier = pltpu.get_barrier_semaphore()
    for ty, tx in peers:
        pl.semaphore_signal(barrier, inc=1, device_id=(ty, tx), device_id_type=MESH)
    pl.semaphore_wait(barrier, len(peers))


def halo_kernel(tile, ext, local, side_send, side_recv, rows_send, rows_recv):
    ty, tx, n, m, up, down, west, east = neighbours()
    cells = tile.shape[1]
    margin = cells // 2
    size = 2 * cells
    far = cells + margin
    greet([(up, tx), (down, tx), (ty, west), (ty, east)])

    core = lax.rem(ty, 2)
    copies = {}
    for step in range(2):
        h = core if step == 0 else 1 - core
        at = pl.multiple_of(h * margin, margin)
        src_rows = pl.ds(at, margin)
        dst_rows = pl.ds(pl.multiple_of(at + margin, margin), margin)
        for side, (peer, src, dst) in enumerate(
            ((east, pl.ds(margin, margin), pl.ds(0, margin)), (west, pl.ds(0, margin), pl.ds(far, margin)))
        ):
            copy = remote(
                tile.at[:, src_rows, src],
                ext.at[:, dst_rows, dst],
                side_send.at[step, side],
                side_recv.at[step, side],
                ty,
                peer,
            )
            copy.start()
            copies[step, side] = copy
    middle = pl.ds(margin, cells)
    to_up = remote(
        tile.at[:, pl.ds(0, margin), :], ext.at[:, pl.ds(far, margin), middle],
        rows_send.at[0, 0], rows_recv.at[0, 0], up, tx,
    )
    to_down = remote(
        tile.at[:, pl.ds(margin, margin), :], ext.at[:, pl.ds(0, margin), middle],
        rows_send.at[1, 0], rows_recv.at[1, 0], down, tx,
    )
    to_up.start()
    to_down.start()
    own = pltpu.make_async_copy(tile, ext.at[:, middle, middle], local)
    own.start()

    sides = (pl.ds(0, margin), pl.ds(far, margin))

    def corner(direction, side):
        if direction == 0:
            src, dst, peer = margin, far, up
        else:
            src, dst, peer = cells, 0, down
        return remote(
            ext.at[:, pl.ds(src, margin), sides[side]],
            ext.at[:, pl.ds(dst, margin), sides[side]],
            rows_send.at[direction, 1 + side],
            rows_recv.at[direction, 1 + side],
            peer,
            tx,
        )

    for step in range(2):
        for side in range(2):
            copies[step, side].wait_recv()
            for direction in range(2):

                @pl.when(core == (direction if step == 0 else 1 - direction))
                def _(direction=direction, side=side):
                    corner(direction, side).start()

    for step in range(2):
        for side in range(2):
            copies[step, side].wait_send()
    own.wait()
    to_up.wait()
    to_down.wait()
    for direction in range(2):
        for side in range(2):
            corner(direction, side).wait()

    for there, rows, cols in (
        (ty == 0, pl.ds(0, margin), pl.ds(0, size)),
        (ty == n - 1, pl.ds(far, margin), pl.ds(0, size)),
        (tx == 0, pl.ds(0, size), pl.ds(0, margin)),
        (tx == m - 1, pl.ds(0, size), pl.ds(far, margin)),
    ):

        @pl.when(there)
        def _(rows=rows, cols=cols):
            ext[:, rows, cols] = jnp.zeros((2, rows.size, cols.size), F32)


def halo(tile):
    cells = tile.shape[1]
    dma = pltpu.SemaphoreType.DMA
    return pl.pallas_call(
        halo_kernel,
        out_shape=jax.ShapeDtypeStruct((2, 2 * cells, 2 * cells), F32),
        in_specs=[VMEM],
        out_specs=VMEM,
        scratch_shapes=[dma(()), dma((2, 2)), dma((2, 2)), dma((2, 3)), dma((2, 3))],
        compiler_params=pltpu.CompilerParams(collective_id=0, has_side_effects=True),
        name="halo",
    )(tile)


def return_kernel(
    grid, part, inner, total,
    from_below, from_above, side_out, from_side, core_in, plane_in, line_in,
    rows_send, rows_recv, side_send, side_recv,
    core_send, core_recv, plane_send, plane_recv, line_send, line_recv,
    back_send, back_recv, pair_send, pair_recv,
):
    ty, tx, n, m, up, down, west, east = neighbours()
    cells = inner.shape[1]
    margin = cells // 2
    far = cells + margin
    core = lax.rem(ty, 2)
    mate = ty + 1 - 2 * core
    chip, lane, line = ty // 2, lax.rem(tx, 2), tx // 2
    plane_size, line_size = n, m // 2
    me = chip * 2 + lane

    def plane_peer(d):
        other = lax.rem(me + d, plane_size)
        return other, (other // 2) * 2 + core, line * 2 + lax.rem(other, 2)

    def line_peer(d):
        return lax.rem(line + d, line_size) * 2 + lane

    peers = [(up, tx), (down, tx), (ty, west), (ty, east)]
    peers.append((mate, tx))
    for d in range(1, plane_size):
        _, py, px = plane_peer(d)
        peers.append((py, px))
    for d in range(1, line_size):
        peers.append((ty, line_peer(d)))
    greet(peers)

    rows = part.shape[0]
    half = rows // 2
    piece = half // plane_size
    mine = pl.multiple_of(core * half, half)
    others = pl.multiple_of((1 - core) * half, half)

    swap = remote(part.at[pl.ds(others, half)], core_in, core_send, core_recv, mate, tx)
    swap.start()

    row_copies = {}
    cols = (pl.ds(0, margin), pl.ds(far, margin), pl.ds(margin, cells))
    for i, at in enumerate(cols):
        for direction, (src, dst, peer) in enumerate(
            ((pl.ds(0, margin), from_below, up), (pl.ds(far, margin), from_above, down))
        ):
            copy = remote(
                grid.at[:, src, at], dst.at[:, :, at], rows_send.at[direction, i], rows_recv.at[direction, i], peer, tx
            )
            copy.start()
            row_copies[direction, i] = copy

    swap.wait()
    core_in[...] = core_in[...] + part[pl.ds(mine, half), :]
    plane_copies = []
    for d in range(1, plane_size):
        other, py, px = plane_peer(d)
        copy = remote(
            core_in.at[pl.ds(pl.multiple_of(other * piece, piece), piece)],
            plane_in.at[d],
            plane_send.at[d],
            plane_recv.at[d],
            py,
            px,
        )
        copy.start()
        plane_copies.append(copy)

    side_copies = []
    for step in range(2):
        for source in range(2):
            lower = source == 0

            @pl.when(core == (source if step == 0 else 1 - source))
            def _(source=source, lower=lower):
                received = from_below if lower else from_above
                edge = ty == (n - 1 if lower else 0)
                src_row = cells if lower else margin
                for side in range(2):
                    row_copies[0 if lower else 1, side].wait_recv()
                    at = cols[side]
                    add = jnp.where(edge, 0.0, received[:, :, at])
                    side_out[side, 1 if lower else 0] = grid[:, pl.ds(src_row, margin), at] + add

        h = 1 - core if step == 0 else core
        for side, peer in ((0, west), (1, east)):
            copy = remote(
                side_out.at[side, h], from_side.at[side, h], side_send.at[side, step], side_recv.at[side, step], ty, peer
            )
            copy.start()
            side_copies.append(copy)

    for copy in plane_copies:
        copy.wait()
    own = core_in[pl.ds(pl.multiple_of(me * piece, piece), piece), :]
    for d in range(1, plane_size):
        own = own + plane_in[d]
    line_in[line] = own
    line_copies = []
    for d in range(1, line_size):
        copy = remote(
            line_in.at[line], line_in.at[line], line_send.at[d], line_recv.at[d], ty, line_peer(d)
        )
        copy.start()
        line_copies.append(copy)
    for copy in line_copies:
        copy.wait()
    done = line_in[0]
    for d in range(1, line_size):
        done = done + line_in[d]

    place = pl.ds(pl.multiple_of(mine + me * piece, piece), piece)
    total[place, :] = done
    back = []
    for d in range(1, plane_size):
        _, py, px = plane_peer(d)
        copy = remote(total.at[place], total.at[place], back_send.at[d], back_recv.at[d], py, px)
        copy.start()
        back.append(copy)
    pair = [remote(total.at[place], total.at[place], pair_send.at[0], pair_recv.at[0], mate, tx)]
    pair[0].start()
    for d in range(1, plane_size):
        back[d - 1].wait_recv()
        source = lax.rem(me + plane_size - d, plane_size)
        at = pl.ds(pl.multiple_of(mine + source * piece, piece), piece)
        copy = remote(total.at[at], total.at[at], pair_send.at[d], pair_recv.at[d], mate, tx)
        copy.start()
        pair.append(copy)

    for direction in range(2):
        row_copies[direction, 2].wait_recv()
    for copy in side_copies:
        copy.wait()
    middle = pl.ds(margin, cells)
    for h in range(2):
        received = from_above if h == 0 else from_below
        edge = ty == (0 if h == 0 else n - 1)
        value = grid[:, pl.ds(margin + h * margin, margin), middle] + jnp.where(edge, 0.0, received[:, :, middle])
        from_west = jnp.where(tx == 0, 0.0, from_side[1, h])
        from_east = jnp.where(tx == m - 1, 0.0, from_side[0, h])
        inner[:, pl.ds(h * margin, margin), :] = value + jnp.concatenate([from_west, from_east], 2)

    for key in row_copies:
        row_copies[key].wait_send()
    for copy in back:
        copy.wait_send()
    for copy in pair:
        copy.wait()


def give_back(grid, part):
    cells = grid.shape[1] // 2
    margin = cells // 2
    rows, width = part.shape
    n, m = lax.axis_size("ty"), lax.axis_size("tx")
    plane, line = n, m // 2
    piece = rows // 2 // plane
    dma = pltpu.SemaphoreType.DMA
    return pl.pallas_call(
        return_kernel,
        out_shape=(
            jax.ShapeDtypeStruct((2, cells, cells), F32),
            jax.ShapeDtypeStruct(part.shape, F32),
        ),
        in_specs=[VMEM, VMEM],
        out_specs=(VMEM, VMEM),
        scratch_shapes=[
            pltpu.VMEM((2, margin, 2 * cells), F32),
            pltpu.VMEM((2, margin, 2 * cells), F32),
            pltpu.VMEM((2, 2, 2, margin, margin), F32),
            pltpu.VMEM((2, 2, 2, margin, margin), F32),
            pltpu.VMEM((rows // 2, width), F32),
            pltpu.VMEM((plane, piece, width), F32),
            pltpu.VMEM((line, piece, width), F32),
            dma((2, 3)), dma((2, 3)), dma((2, 2)), dma((2, 2)),
            dma(()), dma(()), dma((plane,)), dma((plane,)), dma((line,)), dma((line,)),
            dma((plane,)), dma((plane,)), dma((plane,)), dma((plane,)),
        ],
        compiler_params=pltpu.CompilerParams(collective_id=1, has_side_effects=True),
        name="give_back",
    )(grid, part)


def shards(object_field, probe_modes, intensities, offsets, counts):
    ext = halo(object_field)
    grid, part = slots(counts, offsets[0, 0], ext, probe_modes, intensities[0, 0])
    inner, total = give_back(grid, part.reshape(-1, part.shape[-1]))
    count = lax.axis_size("ty") * lax.axis_size("tx")
    return inner, total.reshape(probe_modes.shape) * (1.0 / count)


def solution(mesh):
    placed = (
        P(None, "ty", "tx"),
        P(),
        P("ty", "tx", None, None, None),
        P("ty", "tx", None, None),
        P(),
    )
    return jax.shard_map(
        shards, mesh=mesh, in_specs=placed, out_specs=(P(None, "ty", "tx"), P()), check_vma=False
    )
```

time: 472 us -> 93.9 us (0.20)
  waiting for transfers between devices: 333 us -> 0 us
  Pallas kernels: 0 us -> 88.4 us
  starting transfers between devices: 66 us -> 0 us
  matrix products: 29.9 us -> 0 us
  local copies, waits for them, and re-layouts: 17.3 us -> 2.13 us
  between operations: 14.2 us -> 0.66 us
  loops' own time: 5.13 us -> 0 us
    psum x1 -> x0, waiting for transfers between devices: 295 us -> none  [shards(): probe_total = lax.psum(probe_sum, ('ty', 'tx'))]
    pallas_call x0 -> x3, Pallas kernels: none -> 88.4 us  [the longest x1 52.5 us: give_back(): pl.pallas_call(return_kernel, out_shape=(jax.ShapeDtypeStruct((2, cells,...]
    ppermute x8 -> x0, starting transfers between devices: 66 us -> none  [the longest x4 55 us: shifted(): lax.ppermute(value, axis, [(source, source + steps) for source in range(i...]
    ppermute x8 -> x0, waiting for transfers between devices: 37.6 us -> none  [the longest x2 17.9 us: padded_2(): before = lax.ppermute(last, axis, up)]
    dot_general x16 -> x0, matrix products: 29.9 us -> none  [the longest x2 3.91 us: transform(): jnp.einsum('mkn,nj->mkj', left_imag, sine, precision=exact_mode)]
    dynamic_update_slice x1 -> x0, local copies, waits for them, and re-layouts: 6.46 us -> none  [add_patch(): return lax.dynamic_update_slice(grid, current + part, start)]
    another operation x1 -> x0, loops' own time: 5.13 us -> none  [shards(): grid, probe_sum = lax.fori_loop(0, listed, home_step, start_carry)]
  transfers between devices with their start and end apart: 9 -> 0, of which waited for: 6 -> 0; matrix products, arithmetic and copies ran while one was open for 1% -> 0% of each run, Pallas kernels for 0% -> 0%
where the time goes in v1:
time: 93.9 us; the launch traced here: 93.5 us
  Pallas kernels  88.4 us (94%)
  other arithmetic  2.32 us (2%)
  local copies, waits for them, and re-layouts  2.13 us (2%)
    pallas_call x1, Pallas kernels, give_back(): pl.pallas_call(return_kernel, out_shape=(jax.ShapeDtypeStruct((2, cells,...  52.5 us
    pallas_call x1, Pallas kernels, halo(): pl.pallas_call(halo_kernel, out_shape=jax.ShapeDtypeStruct((2, 2 * cells,...  23.1 us
    pallas_call x1, Pallas kernels, slots(): pl.pallas_call(slots_kernel, out_shape=(jax.ShapeDtypeStruct(ext.shape, F...  12.8 us
    mul x1, other arithmetic, shards(): return (inner, total.reshape(probe_modes.shape) * (1.0 / count))  2.32 us

profile of v1, /device:TPU:1, one launch (start us, length us, event | category | flops | bytes accessed | tf_op | source)
XLA Modules:
  0.0 93.5 jit_solution(5382216946264879433)
XLA Ops:
  0.6 1.3 %copy.13.spots = s32[3,2]{1,0:T(4,128)} copy(s32[3,2]{0,1:T(2,128)} %bitcast.7) | data formatting | bytes 48 | tf_op jit(solution)/shard_map/squeeze | solution.py:499
  2.0 23.1 %halo.1.ext = f32[2,512,512]{2,1,0:T(8,128)} custom-call(f32[2,256,256]{2,1,0:T(8,128)} %tile.1), custom_call_target="tpu_custom_call" | custom-call | tf_op jit(solution)/shard_map/halo/pallas_call | solution.py:301
  25.1 12.8 %slots.1 = (f32[2,512,512]{2,1,0:T(8,128)}, f32[2,2,256,256]{3,2,1,0:T(8,128)}) custom-call(s32[16,16]{1,0:T(8,128)} %counts.1, s32[3,2]{1,0:T(4,128)} %copy.13.spots, f32[2,512,512]{2,1,0:T(8,128)} %halo.1.ext, f32[2,2,256,256]{3,2,1,0:T(8,128)} %probe.1, f32[3,256,256]{2,1,0:T(8,128)} %bitcast.6, bf16[2,768,256]{2,1,0:T(8,128)(2,1)} %constant.14.clone.right, ...), custom_call_target="tpu_custom_call" | custom-call | tf_op jit(solution)/shard_map/slots/pallas_call | solution.py:171
  37.9 52.5 %give_back.1 = (f32[2,256,256]{2,1,0:T(8,128)}, f32[1024,256]{1,0:T(8,128)}) custom-call(f32[2,512,512]{2,1,0:T(8,128)} %get-tuple-element.6.grid, f32[1024,256]{1,0:T(8,128)} %bitcast.4), custom_call_target="tpu_custom_call" | custom-call | tf_op jit(solution)/shard_map/give_back/pallas_call | solution.py:472
  90.4 0.0 copy-start
  90.4 2.3 %broadcast_multiply_fusion = f32[1024,256]{1,0:T(8,128)} fusion(f32[1024,256]{1,0:T(8,128)} %get-tuple-element.9), kind=kLoop, calls=%fused_computation | loop fusion | flops 262144 | bytes 2097152 | tf_op jit(solution)/shard_map/mul | solution.py:502
  92.7 0.0 copy-done
  92.7 0.8 copy.15
Async XLA Ops:
  90.4 2.3 %copy-start = (f32[2,256,256]{2,1,0:T(8,128)S(1)}, f32[2,256,256]{2,1,0:T(8,128)}, u32[]{:S(2)}) copy-start(f32[2,256,256]{2,1,0:T(8,128)} %get-tuple-element.12) | copy-start | bytes 1572868

commit v2 on v0

v2 whole, which is shorter than its diff:
```python
import functools

import jax
import jax.numpy as jnp
import numpy as np
from jax import lax
from jax.experimental import pallas as pl
from jax.experimental.pallas import tpu as pltpu
from jax.sharding import PartitionSpec as P

FLOOR = 0.5
MESH = pl.DeviceIdType.MESH
F32 = jnp.float32
BF16 = jnp.bfloat16
VMEM = pl.BlockSpec(memory_space=pltpu.VMEM)
SMEM = pl.BlockSpec(memory_space=pltpu.SMEM)


def tables(pattern):
    half = pattern // 2
    n = np.arange(half)[:, None]
    out = []
    for parity in (0, 1):
        k = 2 * np.arange(half)[None, :] + parity
        angle = 2.0 * np.pi * ((n * k) % pattern) / pattern
        c, s = np.cos(angle) / np.sqrt(pattern), np.sin(angle) / np.sqrt(pattern)
        full = np.block([[c, -s], [s, c]])
        hi = full.astype(BF16)
        lo = (full - hi.astype(np.float64)).astype(BF16)
        out.append(np.stack([hi, lo]))
    forward = np.stack(out)
    return forward, forward.swapaxes(2, 3)


def reorder_table(pattern):
    half = pattern // 2
    table = np.zeros((pattern, pattern), np.float32)
    table[2 * np.arange(half), np.arange(half)] = 1
    table[2 * np.arange(half) + 1, half + np.arange(half)] = 1
    return table.astype(BF16)


def split(a):
    hi = a.astype(BF16)
    return hi, (a - hi.astype(F32)).astype(BF16)


def times_right(a, table, parity):
    hi, lo = split(a)
    w, v = table[parity, 0], table[parity, 1]
    return jnp.dot(
        jnp.concatenate([hi, lo, hi], axis=1), jnp.concatenate([w, w, v], axis=0), preferred_element_type=F32
    )


def times_left(table, parity, a):
    hi, lo = split(a)
    w, v = table[parity, 0], table[parity, 1]
    return jnp.dot(
        jnp.concatenate([w, w, v], axis=1), jnp.concatenate([hi, lo, hi], axis=0), preferred_element_type=F32
    )


def regroup(a, half):
    re = jnp.concatenate([a[:, :half], a[:, 2 * half : 3 * half]], 1)
    im = jnp.concatenate([a[:, half : 2 * half], a[:, 3 * half :]], 1)
    return jnp.concatenate([re, im], 0)


def reordered_root(measured, order, order_t):
    hi, lo = split(jnp.sqrt(measured))
    root = jnp.dot(hi, order[...], preferred_element_type=F32) + jnp.dot(
        lo, order[...], preferred_element_type=F32
    )
    hi, lo = split(root)
    return jnp.dot(order_t[...], hi, preferred_element_type=F32) + jnp.dot(
        order_t[...], lo, preferred_element_type=F32
    )


def slot_gradient(xr, xi, probe, root, used, forward, backward, factor, add_probe):
    pattern = xr.shape[0]
    half = pattern // 2
    modes = probe.shape[1]
    far = []
    for m in range(modes):
        pr, pi = probe[0, m], probe[1, m]
        wr = pr * xr - pi * xi
        wi = pr * xi + pi * xr
        u = jnp.concatenate([wr[:, :half] + wr[:, half:], wi[:, :half] + wi[:, half:]], 1)
        v = jnp.concatenate([wr[:, :half] - wr[:, half:], wi[:, :half] - wi[:, half:]], 1)
        even = times_right(u, forward, 0)
        odd = times_right(v, forward, 1)
        us = jnp.concatenate([even[:half] + even[half:], odd[:half] + odd[half:]], 1)
        vs = jnp.concatenate([even[:half] - even[half:], odd[:half] - odd[half:]], 1)
        far.append((times_left(backward, 0, regroup(us, half)), times_left(backward, 1, regroup(vs, half))))

    for parity in (0, 1):
        power = 0.0
        for m in range(modes):
            g = far[m][parity]
            power = power + g[:half] * g[:half] + g[half:] * g[half:]
        amplitude = jnp.maximum(jnp.sqrt(power), FLOOR)
        factor[parity] = jnp.where(used, 1.0 - root[parity * half : (parity + 1) * half] / amplitude, 0.0)

    object_r = 0.0
    object_i = 0.0
    for m in range(modes):
        pr, pi = probe[0, m], probe[1, m]
        halves = []
        for parity in (0, 1):
            f = factor[parity]
            g = far[m][parity]
            halves.append(times_left(forward, parity, jnp.concatenate([g[:half] * f, g[half:] * f], 0)))
        top, bottom = halves[0] + halves[1], halves[0] - halves[1]
        k = []
        for parity in (0, 1):
            at = slice(parity * half, (parity + 1) * half)
            z = jnp.concatenate(
                [
                    jnp.concatenate([top[:half, at], top[half:, at]], 1),
                    jnp.concatenate([bottom[:half, at], bottom[half:, at]], 1),
                ],
                0,
            )
            k.append(times_right(z, backward, parity))
        near, off = k[0] + k[1], k[0] - k[1]
        br = jnp.concatenate([near[:, :half], off[:, :half]], 1)
        bi = jnp.concatenate([near[:, half:], off[:, half:]], 1)
        object_r = object_r + pr * br + pi * bi
        object_i = object_i + pr * bi - pi * br
        add_probe(m, xr * br + xi * bi, xr * bi - xi * br)
    return object_r, object_i


def turn(a, amount, axis, unit):
    amount = jnp.broadcast_to(amount, a.shape)
    for k in range(unit.bit_length() - 1):
        a = jnp.where((amount >> k) & 1 == 1, pltpu.roll(a, 1 << k, axis), a)
    return a


def below(shape, axis, amount):
    return lax.broadcasted_iota(jnp.int32, shape, axis) < amount


def rows_in(a, skip):
    a = turn(a, (8 - skip) & 7, 1, 8)
    return jnp.where(below(a[1:].shape, 1, 8 - skip), a[:-1], a[1:])


def rows_out(a, skip):
    a = turn(a, skip, 1, 8)
    zero = jnp.zeros((1,) + a.shape[1:], F32)
    over = jnp.concatenate([zero, a], 0)
    here = jnp.concatenate([a, zero], 0)
    return jnp.where(below(here.shape, 1, skip), over, here)


def cols_in(a, col, half):
    block, rest = lax.div(col, half), lax.rem(col, half)
    a = [a[:, i * half : (i + 1) * half] for i in range(4)]
    block = jnp.broadcast_to(block, a[0].shape)
    blocks = [jnp.where(block == 0, a[i], jnp.where(block == 1, a[i + 1], a[i + 2])) for i in range(2)]
    blocks.append(jnp.where(block == 0, a[2], a[3]))
    blocks = [turn(x, (half - rest) & (half - 1), 1, half) for x in blocks]
    first = below(blocks[0].shape, 1, half - rest)
    return jnp.concatenate([jnp.where(first, blocks[0], blocks[1]), jnp.where(first, blocks[1], blocks[2])], 1)


def cols_out(a, col, half):
    block, rest = lax.div(col, half), lax.rem(col, half)
    blocks = [turn(a[:, i * half : (i + 1) * half], rest, 1, half) for i in range(2)]
    over = below(blocks[0].shape, 1, rest)
    b = [jnp.where(over, 0.0, blocks[0]), jnp.where(over, blocks[0], blocks[1]), jnp.where(over, blocks[1], 0.0)]
    block = jnp.broadcast_to(block, b[0].shape)
    zero, one, two = block == 0, block == 1, block == 2
    return jnp.concatenate(
        [
            jnp.where(zero, b[0], 0.0),
            jnp.where(zero, b[1], jnp.where(one, b[0], 0.0)),
            jnp.where(zero, b[2], jnp.where(one, b[1], b[0])),
            jnp.where(one, b[2], jnp.where(two, b[1], 0.0)),
        ],
        1,
    )


def remote(src, dst, send, recv, ty, tx):
    return pltpu.make_async_remote_copy(
        src_ref=src, dst_ref=dst, send_sem=send, recv_sem=recv, device_id=(ty, tx), device_id_type=MESH
    )


def rows_at(start, size):
    return pl.ds(pl.multiple_of(start, size), size)


def kernel(
    chunks,
    counts, spots, tile, probe_any, measured_any, forward_any, backward_any, order_any, order_t_any,
    inner, total,
    ext, probe, root, forward, backward, order, order_t, factor, placed, part, grid,
    from_below, from_above, side_out, from_side, core_in, plane_in, line_in,
    local, side_send, side_recv, rows_send, rows_recv,
    down_send, down_recv, out_send, out_recv,
    core_send, core_recv, plane_send, plane_recv, line_send, line_recv,
    back_send, back_recv, pair_send, pair_recv,
):
    ty, tx = lax.axis_index("ty"), lax.axis_index("tx")
    n, m = lax.axis_size("ty"), lax.axis_size("tx")
    up, down = lax.rem(ty + n - 1, n), lax.rem(ty + 1, n)
    west, east = lax.rem(tx + m - 1, m), lax.rem(tx + 1, m)
    cells = inner.shape[1]
    margin = cells // 2
    size, far = 2 * cells, cells + margin
    middle = pl.ds(margin, cells)
    edge, inside = margin // 8, cells // 8
    core = lax.rem(ty, 2)
    mate = ty + 1 - 2 * core
    chip, lane, line = ty // 2, lax.rem(tx, 2), tx // 2
    plane_size, line_size = n, m // 2
    me = chip * 2 + lane
    cap = root.shape[0]

    def plane_peer(d):
        other = lax.rem(me + d, plane_size)
        return other, (other // 2) * 2 + core, line * 2 + lax.rem(other, 2)

    def line_peer(d):
        return lax.rem(line + d, line_size) * 2 + lane

    loads = [
        pltpu.make_async_copy(src, dst, local.at[i])
        for i, (src, dst) in enumerate(
            (
                (measured_any.at[0, 0], root),
                (order_any, order),
                (order_t_any, order_t),
                (tile, ext.at[:, pl.ds(edge, inside), :, middle]),
                (probe_any, probe),
                (forward_any, forward),
                (backward_any, backward),
            )
        )
    ]
    for load in loads:
        load.start()

    peers = [(up, tx), (down, tx), (ty, west), (ty, east), (mate, tx)]
    for d in range(1, plane_size):
        peers.append(plane_peer(d)[1:])
    for d in range(1, line_size):
        peers.append((ty, line_peer(d)))
    barrier = pltpu.get_barrier_semaphore()
    for peer in peers:
        pl.semaphore_signal(barrier, inc=1, device_id=peer, device_id_type=MESH)
    pl.semaphore_wait(barrier, len(peers))

    sides = {}
    for step in range(2):
        h = core if step == 0 else 1 - core
        for side, (peer, src, dst) in enumerate(
            ((east, pl.ds(margin, margin), pl.ds(0, margin)), (west, pl.ds(0, margin), pl.ds(far, margin)))
        ):
            copy = remote(
                tile.at[:, pl.ds(h * edge, edge), :, src],
                ext.at[:, pl.ds((h + 1) * edge, edge), :, dst],
                side_send.at[step, side],
                side_recv.at[step, side],
                ty,
                peer,
            )
            copy.start()
            sides[step, side] = copy
    to_up = remote(
        tile.at[:, pl.ds(0, edge)], ext.at[:, pl.ds(3 * edge, edge), :, middle],
        rows_send.at[0, 0], rows_recv.at[0, 0], up, tx,
    )
    to_down = remote(
        tile.at[:, pl.ds(edge, edge)], ext.at[:, pl.ds(0, edge), :, middle],
        rows_send.at[1, 0], rows_recv.at[1, 0], down, tx,
    )
    to_up.start()
    to_down.start()

    placed[...] = jnp.zeros(placed.shape, F32)
    part[...] = jnp.zeros(part.shape, F32)
    ext[:, pl.ds(size // 8, 1)] = jnp.zeros((2, 1, 8, size), F32)
    for load in loads[:3]:
        load.wait()

    @pl.loop(0, cap)
    def _(slot):
        root[slot] = reordered_root(root[slot], order, order_t)

    strips = (pl.ds(0, margin), pl.ds(far, margin))

    def corner(direction, side):
        src, dst, peer = (edge, 3 * edge, up) if direction == 0 else (2 * edge, 0, down)
        return remote(
            ext.at[:, pl.ds(src, edge), :, strips[side]],
            ext.at[:, pl.ds(dst, edge), :, strips[side]],
            rows_send.at[direction, 1 + side],
            rows_recv.at[direction, 1 + side],
            peer,
            tx,
        )

    for step in range(2):
        for side in range(2):
            sides[step, side].wait_recv()
            for direction in range(2):

                @pl.when(core == (direction if step == 0 else 1 - direction))
                def _(direction=direction, side=side):
                    corner(direction, side).start()

    for load in loads[3:]:
        load.wait()
    for copy in sides.values():
        copy.wait_send()
    to_up.wait()
    to_down.wait()
    for direction in range(2):
        for side in range(2):
            corner(direction, side).wait()

    for there, rows, cols in (
        (ty == 0, pl.ds(0, edge), pl.ds(0, size)),
        (ty == n - 1, pl.ds(3 * edge, edge), pl.ds(0, size)),
        (tx == 0, pl.ds(0, size // 8), pl.ds(0, margin)),
        (tx == m - 1, pl.ds(0, size // 8), pl.ds(far, margin)),
    ):

        @pl.when(there)
        def _(rows=rows, cols=cols):
            ext[:, rows, :, cols] = jnp.zeros((2, rows.size, 8, cols.size), F32)

    half = margin
    tall = cells // 8 + 1
    listed = counts[ty, tx]

    def spot(slot):
        row, col = spots[0, 0, slot, 0], spots[0, 0, slot, 1]
        return lax.div(row, 8), lax.rem(row, 8), col

    @pl.loop(0, cap)
    def _(slot):
        group, skip, col = spot(slot)
        used = jnp.broadcast_to(listed, (margin, cells)) > slot

        def window(p):
            strip = ext[p, pl.ds(group, tall)]
            return cols_in(rows_in(strip, skip).reshape(cells, size), col, half)

        def add_probe(mode, re, im):
            for p, value in ((0, re), (1, im)):
                at = pl.ds((p * probe.shape[1] + mode) * cells, cells)
                part[at, :] += value

        pieces = slot_gradient(
            window(0), window(1), probe, root[slot], used, forward, backward, factor, add_probe
        )
        for p, piece in enumerate(pieces):
            piece = cols_out(piece, col, half).reshape(cells // 8, 8, size)
            placed[slot, p, pl.ds(cells // 8, tall)] = rows_out(piece, skip)

    count = part.shape[0] // chunks
    share = count // 2
    piece = share // plane_size
    mine = [c * count + core * share for c in range(chunks)]
    swaps = []
    for c in range(chunks):
        copy = remote(
            part.at[rows_at(c * count + (1 - core) * share, share)],
            core_in.at[c],
            core_send.at[c],
            core_recv.at[c],
            mate,
            tx,
        )
        copy.start()
        swaps.append(copy)

    where = [spot(slot) for slot in range(cap)]

    def assemble(first, height):
        for p in range(2):
            value = 0.0
            for slot, (group, _, _) in enumerate(where):
                value = value + placed[slot, p, pl.ds((cells + first) // 8 - group, height // 8)]
            grid[p, pl.ds(first, height), :] = value.reshape(height, size)

    assemble(0, margin)
    assemble(far, margin)

    row_copies = {}
    cols = (strips[0], strips[1], middle)
    for i, at in enumerate(cols):
        for direction, (src, dst, peer) in enumerate(
            ((pl.ds(0, margin), from_below, up), (pl.ds(far, margin), from_above, down))
        ):
            copy = remote(
                grid.at[:, src, at], dst.at[:, :, at], down_send.at[direction, i], down_recv.at[direction, i], peer, tx
            )
            copy.start()
            row_copies[direction, i] = copy

    plane_copies = []
    for c in range(chunks):
        swaps[c].wait()
        core_in[c] = core_in[c] + part[rows_at(mine[c], share), :]
        copies = []
        for d in range(1, plane_size):
            other, py, px = plane_peer(d)
            copy = remote(
                core_in.at[c, rows_at(other * piece, piece)],
                plane_in.at[c, d],
                plane_send.at[c, d],
                plane_recv.at[c, d],
                py,
                px,
            )
            copy.start()
            copies.append(copy)
        plane_copies.append(copies)

    assemble(margin, cells)

    side_copies = []
    for step in range(2):
        for lower in (True, False):

            @pl.when(core == (0 if lower == (step == 0) else 1))
            def _(lower=lower):
                received = from_below if lower else from_above
                outer = ty == (n - 1 if lower else 0)
                for side in range(2):
                    row_copies[0 if lower else 1, side].wait_recv()
                    at = cols[side]
                    add = jnp.where(outer, 0.0, received[:, :, at])
                    side_out[side, 1 if lower else 0] = grid[:, pl.ds(cells if lower else margin, margin), at] + add

        h = 1 - core if step == 0 else core
        for side, peer in ((0, west), (1, east)):
            copy = remote(
                side_out.at[side, h], from_side.at[side, h], out_send.at[side, step], out_recv.at[side, step], ty, peer
            )
            copy.start()
            side_copies.append(copy)

    line_copies = []
    for c in range(chunks):
        for copy in plane_copies[c]:
            copy.wait()
        own = core_in[c, rows_at(me * piece, piece), :]
        for d in range(1, plane_size):
            own = own + plane_in[c, d]
        line_in[c, line] = own
        copies = []
        for d in range(1, line_size):
            copy = remote(
                line_in.at[c, line], line_in.at[c, line], line_send.at[c, d], line_recv.at[c, d], ty, line_peer(d)
            )
            copy.start()
            copies.append(copy)
        line_copies.append(copies)

    backs, pairs = [], []
    for c in range(chunks):
        for copy in line_copies[c]:
            copy.wait()
        done = line_in[c, 0]
        for d in range(1, line_size):
            done = done + line_in[c, d]
        place = rows_at(mine[c] + me * piece, piece)
        total[place, :] = done * (1.0 / (n * m))
        copies = []
        for d in range(1, plane_size):
            _, py, px = plane_peer(d)
            copy = remote(total.at[place], total.at[place], back_send.at[c, d], back_recv.at[c, d], py, px)
            copy.start()
            copies.append(copy)
        backs.append(copies)
        copy = remote(total.at[place], total.at[place], pair_send.at[c, 0], pair_recv.at[c, 0], mate, tx)
        copy.start()
        pairs.append(copy)

    for direction in range(2):
        row_copies[direction, 2].wait_recv()
    for copy in side_copies:
        copy.wait()
    for h in range(2):
        received = from_above if h == 0 else from_below
        outer = ty == (0 if h == 0 else n - 1)
        value = grid[:, pl.ds((h + 1) * margin, margin), middle] + jnp.where(outer, 0.0, received[:, :, middle])
        from_west = jnp.where(tx == 0, 0.0, from_side[1, h])
        from_east = jnp.where(tx == m - 1, 0.0, from_side[0, h])
        inner[:, pl.ds(h * margin, margin), :] = value + jnp.concatenate([from_west, from_east], 2)
    for copy in row_copies.values():
        copy.wait_send()

    for c in range(chunks):
        for d in range(1, plane_size):
            backs[c][d - 1].wait_recv()
            source = lax.rem(me + plane_size - d, plane_size)
            at = rows_at(mine[c] + source * piece, piece)
            copy = remote(total.at[at], total.at[at], pair_send.at[c, d], pair_recv.at[c, d], mate, tx)
            copy.start()
            pairs.append(copy)
    for copies in backs:
        for copy in copies:
            copy.wait_send()
    for copy in pairs:
        copy.wait()


def shards(object_field, probe_modes, intensities, offsets, counts):
    chunks = 2
    cells = object_field.shape[1]
    margin, size = cells // 2, 2 * cells
    modes = probe_modes.shape[1]
    cap = intensities.shape[2]
    rows = 2 * modes * cells
    plane, line = lax.axis_size("ty"), lax.axis_size("tx") // 2
    share = rows // chunks // 2
    piece = share // plane
    forward, backward = tables(cells)
    order = reorder_table(cells)
    dma = pltpu.SemaphoreType.DMA
    vmem = pltpu.VMEM
    anywhere = pl.BlockSpec(memory_space=pl.ANY)
    inner, total = pl.pallas_call(
        functools.partial(kernel, chunks),
        out_shape=(jax.ShapeDtypeStruct((2, cells, cells), F32), jax.ShapeDtypeStruct((rows, cells), F32)),
        in_specs=[SMEM, SMEM] + [anywhere] * 7,
        out_specs=(VMEM, VMEM),
        scratch_shapes=[
            vmem((2, size // 8 + 1, 8, size), F32),
            vmem(probe_modes.shape, F32),
            vmem((cap, cells, cells), F32),
            vmem(forward.shape, BF16),
            vmem(backward.shape, BF16),
            vmem(order.shape, BF16),
            vmem(order.shape, BF16),
            vmem((2, margin, cells), F32),
            vmem((cap, 2, 3 * cells // 8, 8, size), F32),
            vmem((rows, cells), F32),
            vmem((2, size, size), F32),
            vmem((2, margin, size), F32),
            vmem((2, margin, size), F32),
            vmem((2, 2, 2, margin, margin), F32),
            vmem((2, 2, 2, margin, margin), F32),
            vmem((chunks, share, cells), F32),
            vmem((chunks, plane, piece, cells), F32),
            vmem((chunks, line, piece, cells), F32),
            dma((7,)),
            dma((2, 2)), dma((2, 2)), dma((2, 3)), dma((2, 3)),
            dma((2, 3)), dma((2, 3)), dma((2, 2)), dma((2, 2)),
            dma((chunks,)), dma((chunks,)),
            dma((chunks, plane)), dma((chunks, plane)), dma((chunks, line)), dma((chunks, line)),
            dma((chunks, plane)), dma((chunks, plane)), dma((chunks, plane)), dma((chunks, plane)),
        ],
        compiler_params=pltpu.CompilerParams(collective_id=0, has_side_effects=True),
        name="gradient",
    )(
        counts, offsets, object_field.reshape(2, cells // 8, 8, cells), probe_modes, intensities,
        jnp.asarray(forward), jnp.asarray(backward), jnp.asarray(order), jnp.asarray(order.T),
    )
    return inner, total.reshape(probe_modes.shape)


def solution(mesh):
    placed = (
        P(None, "ty", "tx"),
        P(),
        P("ty", "tx", None, None, None),
        P("ty", "tx", None, None),
        P(),
    )
    return jax.shard_map(
        shards, mesh=mesh, in_specs=placed, out_specs=(P(None, "ty", "tx"), P()), check_vma=False
    )
```

time: 472 us -> 92.5 us (0.20)
  waiting for transfers between devices: 333 us -> 0 us
  Pallas kernels: 0 us -> 87.4 us
  starting transfers between devices: 66 us -> 0 us
  matrix products: 29.9 us -> 0 us
  between operations: 14.2 us -> 0.66 us
  local copies, waits for them, and re-layouts: 17.3 us -> 4.27 us
  other arithmetic: 6.86 us -> 0 us
  loops' own time: 5.13 us -> 0 us
    psum x1 -> x0, waiting for transfers between devices: 295 us -> none  [shards(): probe_total = lax.psum(probe_sum, ('ty', 'tx'))]
    pallas_call x0 -> x1, Pallas kernels: none -> 87.4 us  [shards(): pl.pallas_call(functools.partial(kernel, chunks), out_shape=(jax.ShapeDty...]
    ppermute x8 -> x0, starting transfers between devices: 66 us -> none  [the longest x4 55 us: shifted(): lax.ppermute(value, axis, [(source, source + steps) for source in range(i...]
    ppermute x8 -> x0, waiting for transfers between devices: 37.6 us -> none  [the longest x2 17.9 us: padded_2(): before = lax.ppermute(last, axis, up)]
    dot_general x16 -> x0, matrix products: 29.9 us -> none  [the longest x2 3.91 us: transform(): jnp.einsum('mkn,nj->mkj', left_imag, sine, precision=exact_mode)]
    dynamic_update_slice x1 -> x0, local copies, waits for them, and re-layouts: 6.46 us -> none  [add_patch(): return lax.dynamic_update_slice(grid, current + part, start)]
    another operation x1 -> x0, loops' own time: 5.13 us -> none  [shards(): grid, probe_sum = lax.fori_loop(0, listed, home_step, start_carry)]
  transfers between devices with their start and end apart: 9 -> 0, of which waited for: 6 -> 0; matrix products, arithmetic and copies ran while one was open for 1% -> 0% of each run, Pallas kernels for 0% -> 0%
where the time goes in v2:
time: 92.5 us; the launch traced here: 92.3 us
  Pallas kernels  87.4 us (94%)
  local copies, waits for them, and re-layouts  4.27 us (5%)
    pallas_call x1, Pallas kernels, shards(): pl.pallas_call(functools.partial(kernel, chunks), out_shape=(jax.ShapeDty...  87.4 us
    unnamed x7, local copies, waits for them, and re-layouts  4.27 us

profile of v2, /device:TPU:1, one launch (start us, length us, event | category | flops | bytes accessed | tf_op | source)
XLA Modules:
  0.0 92.3 jit_solution(13512128677701553818)
XLA Ops:
  0.6 0.0 copy-start.1
  0.6 0.7 copy-done.1
  1.3 0.7 copy.11.spots
  2.0 87.4 %gradient.1 = (f32[2,256,256]{2,1,0:T(8,128)}, f32[1024,256]{1,0:T(8,128)}) custom-call(s32[16,16]{1,0:T(8,128)} %counts.1, s32[1,1,3,2]{3,2,1,0:T(4,128)} %copy.11.spots, f32[2,32,8,256]{3,2,1,0:T(8,128)} %bitcast.3, f32[2,2,256,256]{3,2,1,0:T(8,128)} %probe_any.1, f32[1,1,3,256,256]{4,3,2,1,0:T(8,128)} %measured_any.1, ...), custom_call_target="tpu_custom_call" | custom-call | tf_op jit(solution)/shard_map/gradient/pallas_call | solution.py:534
  89.4 0.0 copy-start
  89.4 2.0 %copy.14 = f32[2,256,256]{2,1,0:T(8,128)} copy(f32[2,256,256]{2,1,0:T(8,128)} %get-tuple-element.8) | data formatting | bytes 1048576
  91.4 0.0 copy-done
  91.4 1.0 %copy.15 = f32[2,2,256,256]{3,2,1,0:T(8,128)} copy(f32[2,2,256,256]{3,2,1,0:T(8,128)S(1)} %bitcast.2) | data formatting | bytes 2097152
Async XLA Ops:
  0.6 0.7 copy-start.1
  89.4 2.0 %copy-start = (f32[1024,256]{1,0:T(8,128)S(1)}, f32[1024,256]{1,0:T(8,128)}, u32[]{:S(2)}) copy-start(f32[1024,256]{1,0:T(8,128)} %get-tuple-element.5) | copy-start | bytes 3145732

commit v3 on v2

--- a/solution.py
+++ b/solution.py
@@ -134,10 +134,7 @@
 
 
 def turn(a, amount, axis, unit):
-    amount = jnp.broadcast_to(amount, a.shape)
-    for k in range(unit.bit_length() - 1):
-        a = jnp.where((amount >> k) & 1 == 1, pltpu.roll(a, 1 << k, axis), a)
-    return a
+    return pltpu.roll(a, amount, axis)
 
 
 def below(shape, axis, amount):
@@ -192,17 +189,24 @@
     )
 
 
+def when(there, *steps):
+    @pl.when(there)
+    def _():
+        for step in steps:
+            step()
+
+
 def rows_at(start, size):
     return pl.ds(pl.multiple_of(start, size), size)
 
 
 def kernel(
     chunks,
-    counts, spots, tile, probe_any, measured_any, forward_any, backward_any, order_any, order_t_any,
+    counts_any, spots_any, tile, probe_any, measured_any, forward_any, backward_any, order_any, order_t_any,
     inner, total,
     ext, probe, root, forward, backward, order, order_t, factor, placed, part, grid,
     from_below, from_above, side_out, from_side, core_in, plane_in, line_in,
-    local, side_send, side_recv, rows_send, rows_recv,
+    pieces_v, counts, spots, local, side_send, side_recv, rows_send, rows_recv,
     down_send, down_recv, out_send, out_recv,
     core_send, core_recv, plane_send, plane_recv, line_send, line_recv,
     back_send, back_recv, pair_send, pair_recv,
@@ -222,6 +226,7 @@
     plane_size, line_size = n, m // 2
     me = chip * 2 + lane
     cap = root.shape[0]
+    has_up, has_down, has_west, has_east = ty > 0, ty < n - 1, tx > 0, tx < m - 1
 
     def plane_peer(d):
         other = lax.rem(me + d, plane_size)
@@ -241,6 +246,8 @@
                 (probe_any, probe),
                 (forward_any, forward),
                 (backward_any, backward),
+                (counts_any, counts),
+                (spots_any, spots),
             )
         )
     ]
@@ -271,7 +278,7 @@
                 ty,
                 peer,
             )
-            copy.start()
+            when(has_east if side == 0 else has_west, copy.start)
             sides[step, side] = copy
     to_up = remote(
         tile.at[:, pl.ds(0, edge)], ext.at[:, pl.ds(3 * edge, edge), :, middle],
@@ -281,12 +288,23 @@
         tile.at[:, pl.ds(edge, edge)], ext.at[:, pl.ds(0, edge), :, middle],
         rows_send.at[1, 0], rows_recv.at[1, 0], down, tx,
     )
-    to_up.start()
-    to_down.start()
+    when(has_up, to_up.start)
+    when(has_down, to_down.start)
 
     placed[...] = jnp.zeros(placed.shape, F32)
     part[...] = jnp.zeros(part.shape, F32)
     ext[:, pl.ds(size // 8, 1)] = jnp.zeros((2, 1, 8, size), F32)
+    for there, rows, cols in (
+        (has_up, pl.ds(0, edge), pl.ds(0, size)),
+        (has_down, pl.ds(3 * edge, edge), pl.ds(0, size)),
+        (has_west, pl.ds(0, size // 8), pl.ds(0, margin)),
+        (has_east, pl.ds(0, size // 8), pl.ds(far, margin)),
+    ):
+
+        @pl.when(jnp.logical_not(there))
+        def _(rows=rows, cols=cols):
+            ext[:, rows, :, cols] = jnp.zeros((2, rows.size, 8, cols.size), F32)
+
     for load in loads[:3]:
         load.wait()
 
@@ -307,35 +325,24 @@
             tx,
         )
 
+    has_side, has_row = (has_west, has_east), (has_up, has_down)
     for step in range(2):
         for side in range(2):
-            sides[step, side].wait_recv()
+            when(has_side[side], sides[step, side].wait_recv)
             for direction in range(2):
-
-                @pl.when(core == (direction if step == 0 else 1 - direction))
-                def _(direction=direction, side=side):
-                    corner(direction, side).start()
+                turn_now = core == (direction if step == 0 else 1 - direction)
+                when(turn_now & has_side[side] & has_row[direction], corner(direction, side).start)
 
     for load in loads[3:]:
         load.wait()
-    for copy in sides.values():
-        copy.wait_send()
-    to_up.wait()
-    to_down.wait()
-    for direction in range(2):
+    for (_, side), copy in sides.items():
+        when(has_side[1 - side], copy.wait_send)
+    for direction, copy in ((0, to_up), (1, to_down)):
+        when(has_row[direction], copy.wait_send)
+        when(has_row[1 - direction], copy.wait_recv)
         for side in range(2):
-            corner(direction, side).wait()
-
-    for there, rows, cols in (
-        (ty == 0, pl.ds(0, edge), pl.ds(0, size)),
-        (ty == n - 1, pl.ds(3 * edge, edge), pl.ds(0, size)),
-        (tx == 0, pl.ds(0, size // 8), pl.ds(0, margin)),
-        (tx == m - 1, pl.ds(0, size // 8), pl.ds(far, margin)),
-    ):
-
-        @pl.when(there)
-        def _(rows=rows, cols=cols):
-            ext[:, rows, :, cols] = jnp.zeros((2, rows.size, 8, cols.size), F32)
+            when(has_row[direction] & has_side[side], corner(direction, side).wait_send)
+            when(has_row[1 - direction] & has_side[side], corner(direction, side).wait_recv)
 
     half = margin
     tall = cells // 8 + 1
@@ -363,8 +370,7 @@
             window(0), window(1), probe, root[slot], used, forward, backward, factor, add_probe
         )
         for p, piece in enumerate(pieces):
-            piece = cols_out(piece, col, half).reshape(cells // 8, 8, size)
-            placed[slot, p, pl.ds(cells // 8, tall)] = rows_out(piece, skip)
+            pieces_v[slot, p] = piece
 
     count = part.shape[0] // chunks
     share = count // 2
@@ -383,6 +389,13 @@
         copy.start()
         swaps.append(copy)
 
+    @pl.loop(0, cap)
+    def _(slot):
+        _, skip, col = spot(slot)
+        for p in range(2):
+            piece = cols_out(pieces_v[slot, p], col, half).reshape(cells // 8, 8, size)
+            placed[slot, p, pl.ds(cells // 8, tall)] = rows_out(piece, skip)
+
     where = [spot(slot) for slot in range(cap)]
 
     def assemble(first, height):
@@ -404,7 +417,7 @@
             copy = remote(
                 grid.at[:, src, at], dst.at[:, :, at], down_send.at[direction, i], down_recv.at[direction, i], peer, tx
             )
-            copy.start()
+            when(has_row[direction], copy.start)
             row_copies[direction, i] = copy
 
     plane_copies = []
@@ -435,9 +448,9 @@
             @pl.when(core == (0 if lower == (step == 0) else 1))
             def _(lower=lower):
                 received = from_below if lower else from_above
-                outer = ty == (n - 1 if lower else 0)
+                outer = jnp.logical_not(has_down if lower else has_up)
                 for side in range(2):
-                    row_copies[0 if lower else 1, side].wait_recv()
+                    when(has_down if lower else has_up, row_copies[0 if lower else 1, side].wait_recv)
                     at = cols[side]
                     add = jnp.where(outer, 0.0, received[:, :, at])
                     side_out[side, 1 if lower else 0] = grid[:, pl.ds(cells if lower else margin, margin), at] + add
@@ -447,8 +460,8 @@
             copy = remote(
                 side_out.at[side, h], from_side.at[side, h], out_send.at[side, step], out_recv.at[side, step], ty, peer
             )
-            copy.start()
-            side_copies.append(copy)
+            when(has_side[side], copy.start)
+            side_copies.append((side, copy))
 
     line_copies = []
     for c in range(chunks):
@@ -488,18 +501,19 @@
         pairs.append(copy)
 
     for direction in range(2):
-        row_copies[direction, 2].wait_recv()
-    for copy in side_copies:
-        copy.wait()
+        when(has_row[1 - direction], row_copies[direction, 2].wait_recv)
+    for side, copy in side_copies:
+        when(has_side[side], copy.wait_send)
+        when(has_side[1 - side], copy.wait_recv)
     for h in range(2):
         received = from_above if h == 0 else from_below
-        outer = ty == (0 if h == 0 else n - 1)
+        outer = jnp.logical_not(has_up if h == 0 else has_down)
         value = grid[:, pl.ds((h + 1) * margin, margin), middle] + jnp.where(outer, 0.0, received[:, :, middle])
-        from_west = jnp.where(tx == 0, 0.0, from_side[1, h])
-        from_east = jnp.where(tx == m - 1, 0.0, from_side[0, h])
+        from_west = jnp.where(has_west, from_side[1, h], 0.0)
+        from_east = jnp.where(has_east, from_side[0, h], 0.0)
         inner[:, pl.ds(h * margin, margin), :] = value + jnp.concatenate([from_west, from_east], 2)
-    for copy in row_copies.values():
-        copy.wait_send()
+    for (direction, _), copy in row_copies.items():
+        when(has_row[direction], copy.wait_send)
 
     for c in range(chunks):
         for d in range(1, plane_size):
@@ -530,11 +544,11 @@
     order = reorder_table(cells)
     dma = pltpu.SemaphoreType.DMA
     vmem = pltpu.VMEM
-    anywhere = pl.BlockSpec(memory_space=pl.ANY)
+    anywhere = pl.BlockSpec(memory_space=pltpu.HBM)
     inner, total = pl.pallas_call(
         functools.partial(kernel, chunks),
         out_shape=(jax.ShapeDtypeStruct((2, cells, cells), F32), jax.ShapeDtypeStruct((rows, cells), F32)),
-        in_specs=[SMEM, SMEM] + [anywhere] * 7,
+        in_specs=[anywhere] * 9,
         out_specs=(VMEM, VMEM),
         scratch_shapes=[
             vmem((2, size // 8 + 1, 8, size), F32),
@@ -555,7 +569,10 @@
             vmem((chunks, share, cells), F32),
             vmem((chunks, plane, piece, cells), F32),
             vmem((chunks, line, piece, cells), F32),
-            dma((7,)),
+            vmem((cap, 2, cells, cells), F32),
+            pltpu.SMEM((plane, 2 * line), jnp.int32),
+            pltpu.SMEM((1, 1, cap, 2), jnp.int32),
+            dma((9,)),
             dma((2, 2)), dma((2, 2)), dma((2, 3)), dma((2, 3)),
             dma((2, 3)), dma((2, 3)), dma((2, 2)), dma((2, 2)),
             dma((chunks,)), dma((chunks,)),

time: 92.5 us -> 80.6 us (0.87)
  Pallas kernels: 87.4 us -> 75.6 us
    pallas_call x1, Pallas kernels: 87.4 us -> 75.6 us  [shards(): pl.pallas_call(functools.partial(kernel, chunks), out_shape=(jax.ShapeDty...]
where the time goes in v3:
time: 80.6 us; the launch traced here: 80.5 us
  Pallas kernels  75.6 us (94%)
  local copies, waits for them, and re-layouts  4.27 us (5%)
    pallas_call x1, Pallas kernels, shards(): pl.pallas_call(functools.partial(kernel, chunks), out_shape=(jax.ShapeDty...  75.6 us
    unnamed x7, local copies, waits for them, and re-layouts  4.27 us

profile of v3, /device:TPU:1, one launch (start us, length us, event | category | flops | bytes accessed | tf_op | source)
XLA Modules:
  0.0 80.5 jit_solution(4486180966813171832)
XLA Ops:
  0.6 0.0 copy-start.1
  0.6 0.7 copy-done.1
  1.3 0.7 copy.11.spots_any
  2.0 75.6 %gradient.1 = (f32[2,256,256]{2,1,0:T(8,128)}, f32[1024,256]{1,0:T(8,128)}) custom-call(s32[16,16]{1,0:T(8,128)} %counts_any.1, s32[1,1,3,2]{3,2,1,0:T(4,128)} %copy.11.spots_any, f32[2,32,8,256]{3,2,1,0:T(8,128)} %bitcast.3, f32[2,2,256,256]{3,2,1,0:T(8,128)} %probe_any.1, f32[1,1,3,256,256]{4,3,2,1,0:T(8,128)} %measured_any.1, ...), custom_call_target="tpu_custom_call" | custom-call | tf_op jit(solution)/shard_map/gradient/pallas_call | solution.py:548
  77.5 0.0 copy-start
  77.5 2.0 %copy.14 = f32[2,256,256]{2,1,0:T(8,128)} copy(f32[2,256,256]{2,1,0:T(8,128)} %get-tuple-element.8) | data formatting | bytes 1048576
  79.5 0.0 copy-done
  79.5 1.0 %copy.15 = f32[2,2,256,256]{3,2,1,0:T(8,128)} copy(f32[2,2,256,256]{3,2,1,0:T(8,128)S(1)} %bitcast.2) | data formatting | bytes 2097152
Async XLA Ops:
  0.6 0.7 copy-start.1
  77.5 2.0 %copy-start = (f32[1024,256]{1,0:T(8,128)S(1)}, f32[1024,256]{1,0:T(8,128)}, u32[]{:S(2)}) copy-start(f32[1024,256]{1,0:T(8,128)} %get-tuple-element.5) | copy-start | bytes 3145732

commit v4 on v3

--- a/solution.py
+++ b/solution.py
@@ -1,5 +1,3 @@
-import functools
-
 import jax
 import jax.numpy as jnp
 import numpy as np
@@ -78,11 +76,10 @@
     )
 
 
-def slot_gradient(xr, xi, probe, root, used, forward, backward, factor, add_probe):
-    pattern = xr.shape[0]
-    half = pattern // 2
+def to_far(xr, xi, probe, root, used, forward, backward, far, factor):
+    half = xr.shape[0] // 2
     modes = probe.shape[1]
-    far = []
+    power = [0.0, 0.0]
     for m in range(modes):
         pr, pi = probe[0, m], probe[1, m]
         wr = pr * xr - pi * xi
@@ -93,44 +90,38 @@
         odd = times_right(v, forward, 1)
         us = jnp.concatenate([even[:half] + even[half:], odd[:half] + odd[half:]], 1)
         vs = jnp.concatenate([even[:half] - even[half:], odd[:half] - odd[half:]], 1)
-        far.append((times_left(backward, 0, regroup(us, half)), times_left(backward, 1, regroup(vs, half))))
-
+        for parity, x in ((0, us), (1, vs)):
+            g = times_left(backward, parity, regroup(x, half))
+            far[m, parity] = g
+            power[parity] = power[parity] + g[:half] * g[:half] + g[half:] * g[half:]
     for parity in (0, 1):
-        power = 0.0
-        for m in range(modes):
-            g = far[m][parity]
-            power = power + g[:half] * g[:half] + g[half:] * g[half:]
-        amplitude = jnp.maximum(jnp.sqrt(power), FLOOR)
+        amplitude = jnp.maximum(jnp.sqrt(power[parity]), FLOOR)
         factor[parity] = jnp.where(used, 1.0 - root[parity * half : (parity + 1) * half] / amplitude, 0.0)
 
-    object_r = 0.0
-    object_i = 0.0
-    for m in range(modes):
-        pr, pi = probe[0, m], probe[1, m]
-        halves = []
-        for parity in (0, 1):
-            f = factor[parity]
-            g = far[m][parity]
-            halves.append(times_left(forward, parity, jnp.concatenate([g[:half] * f, g[half:] * f], 0)))
-        top, bottom = halves[0] + halves[1], halves[0] - halves[1]
-        k = []
-        for parity in (0, 1):
-            at = slice(parity * half, (parity + 1) * half)
-            z = jnp.concatenate(
-                [
-                    jnp.concatenate([top[:half, at], top[half:, at]], 1),
-                    jnp.concatenate([bottom[:half, at], bottom[half:, at]], 1),
-                ],
-                0,
-            )
-            k.append(times_right(z, backward, parity))
-        near, off = k[0] + k[1], k[0] - k[1]
-        br = jnp.concatenate([near[:, :half], off[:, :half]], 1)
-        bi = jnp.concatenate([near[:, half:], off[:, half:]], 1)
-        object_r = object_r + pr * br + pi * bi
-        object_i = object_i + pr * bi - pi * br
-        add_probe(m, xr * br + xi * bi, xr * bi - xi * br)
-    return object_r, object_i
+
+def from_far(far, factor, forward, backward):
+    half = factor.shape[1]
+    halves = []
+    for parity in (0, 1):
+        f, g = factor[parity], far[parity]
+        halves.append(times_left(forward, parity, jnp.concatenate([g[:half] * f, g[half:] * f], 0)))
+    top, bottom = halves[0] + halves[1], halves[0] - halves[1]
+    k = []
+    for parity in (0, 1):
+        at = slice(parity * half, (parity + 1) * half)
+        z = jnp.concatenate(
+            [
+                jnp.concatenate([top[:half, at], top[half:, at]], 1),
+                jnp.concatenate([bottom[:half, at], bottom[half:, at]], 1),
+            ],
+            0,
+        )
+        k.append(times_right(z, backward, parity))
+    near, off = k[0] + k[1], k[0] - k[1]
+    return (
+        jnp.concatenate([near[:, :half], off[:, :half]], 1),
+        jnp.concatenate([near[:, half:], off[:, half:]], 1),
+    )
 
 
 def turn(a, amount, axis, unit):
@@ -201,12 +192,11 @@
 
 
 def kernel(
-    chunks,
     counts_any, spots_any, tile, probe_any, measured_any, forward_any, backward_any, order_any, order_t_any,
     inner, total,
     ext, probe, root, forward, backward, order, order_t, factor, placed, part, grid,
     from_below, from_above, side_out, from_side, core_in, plane_in, line_in,
-    pieces_v, counts, spots, local, side_send, side_recv, rows_send, rows_recv,
+    pieces_v, patch, far_v, counts, spots, local, side_send, side_recv, rows_send, rows_recv,
     down_send, down_recv, out_send, out_recv,
     core_send, core_recv, plane_send, plane_recv, line_send, line_recv,
     back_send, back_recv, pair_send, pair_recv,
@@ -349,7 +339,7 @@
     listed = counts[ty, tx]
 
     def spot(slot):
-        row, col = spots[0, 0, slot, 0], spots[0, 0, slot, 1]
+        row, col = spots[0, 0, 0, slot], spots[0, 0, 1, slot]
         return lax.div(row, 8), lax.rem(row, 8), col
 
     @pl.loop(0, cap)
@@ -361,33 +351,67 @@
             strip = ext[p, pl.ds(group, tall)]
             return cols_in(rows_in(strip, skip).reshape(cells, size), col, half)
 
-        def add_probe(mode, re, im):
-            for p, value in ((0, re), (1, im)):
-                at = pl.ds((p * probe.shape[1] + mode) * cells, cells)
-                part[at, :] += value
-
-        pieces = slot_gradient(
-            window(0), window(1), probe, root[slot], used, forward, backward, factor, add_probe
+        patch[slot, 0], patch[slot, 1] = window(0), window(1)
+        to_far(
+            patch[slot, 0], patch[slot, 1], probe, root[slot], used, forward, backward,
+            far_v.at[slot], factor.at[slot],
         )
-        for p, piece in enumerate(pieces):
-            pieces_v[slot, p] = piece
-
+
+    chunks = probe.shape[1]
     count = part.shape[0] // chunks
     share = count // 2
     piece = share // plane_size
     mine = [c * count + core * share for c in range(chunks)]
-    swaps = []
+    swaps, plane_copies = [], []
     for c in range(chunks):
-        copy = remote(
-            part.at[rows_at(c * count + (1 - core) * share, share)],
-            core_in.at[c],
-            core_send.at[c],
-            core_recv.at[c],
-            mate,
-            tx,
+        swaps.append(
+            remote(
+                part.at[rows_at(c * count + (1 - core) * share, share)],
+                core_in.at[c],
+                core_send.at[c],
+                core_recv.at[c],
+                mate,
+                tx,
+            )
         )
-        copy.start()
-        swaps.append(copy)
+        copies = []
+        for d in range(1, plane_size):
+            other, py, px = plane_peer(d)
+            copies.append(
+                remote(
+                    core_in.at[c, rows_at(other * piece, piece)],
+                    plane_in.at[c, d],
+                    plane_send.at[c, d],
+                    plane_recv.at[c, d],
+                    py,
+                    px,
+                )
+            )
+        plane_copies.append(copies)
+
+    def to_plane(c):
+        swaps[c].wait()
+        core_in[c] = core_in[c] + part[rows_at(mine[c], share), :]
+        for copy in plane_copies[c]:
+            copy.start()
+
+    for mode in range(chunks):
+
+        @pl.loop(0, cap)
+        def _(slot, mode=mode):
+            if mode > 0:
+                when(slot == cap - 1, lambda: to_plane(mode - 1))
+            br, bi = from_far(far_v.at[slot, mode], factor.at[slot], forward, backward)
+            xr, xi = patch[slot, 0], patch[slot, 1]
+            pr, pi = probe[0, mode], probe[1, mode]
+            for p, value in ((0, xr * br + xi * bi), (1, xr * bi - xi * br)):
+                part[pl.ds((mode * 2 + p) * cells, cells), :] += value
+            for p, value in ((0, pr * br + pi * bi), (1, pr * bi - pi * br)):
+                if mode > 0:
+                    value = value + pieces_v[slot, p]
+                pieces_v[slot, p] = value
+
+        swaps[mode].start()
 
     @pl.loop(0, cap)
     def _(slot):
@@ -407,6 +431,7 @@
 
     assemble(0, margin)
     assemble(far, margin)
+    to_plane(chunks - 1)
 
     row_copies = {}
     cols = (strips[0], strips[1], middle)
@@ -420,51 +445,11 @@
             when(has_row[direction], copy.start)
             row_copies[direction, i] = copy
 
-    plane_copies = []
-    for c in range(chunks):
-        swaps[c].wait()
-        core_in[c] = core_in[c] + part[rows_at(mine[c], share), :]
-        copies = []
-        for d in range(1, plane_size):
-            other, py, px = plane_peer(d)
-            copy = remote(
-                core_in.at[c, rows_at(other * piece, piece)],
-                plane_in.at[c, d],
-                plane_send.at[c, d],
-                plane_recv.at[c, d],
-                py,
-                px,
-            )
-            copy.start()
-            copies.append(copy)
-        plane_copies.append(copies)
-
     assemble(margin, cells)
 
-    side_copies = []
-    for step in range(2):
-        for lower in (True, False):
-
-            @pl.when(core == (0 if lower == (step == 0) else 1))
-            def _(lower=lower):
-                received = from_below if lower else from_above
-                outer = jnp.logical_not(has_down if lower else has_up)
-                for side in range(2):
-                    when(has_down if lower else has_up, row_copies[0 if lower else 1, side].wait_recv)
-                    at = cols[side]
-                    add = jnp.where(outer, 0.0, received[:, :, at])
-                    side_out[side, 1 if lower else 0] = grid[:, pl.ds(cells if lower else margin, margin), at] + add
-
-        h = 1 - core if step == 0 else core
-        for side, peer in ((0, west), (1, east)):
-            copy = remote(
-                side_out.at[side, h], from_side.at[side, h], out_send.at[side, step], out_recv.at[side, step], ty, peer
-            )
-            when(has_side[side], copy.start)
-            side_copies.append((side, copy))
-
     line_copies = []
-    for c in range(chunks):
+
+    def to_line(c):
         for copy in plane_copies[c]:
             copy.wait()
         own = core_in[c, rows_at(me * piece, piece), :]
@@ -479,6 +464,32 @@
             copy.start()
             copies.append(copy)
         line_copies.append(copies)
+
+    side_copies = []
+    for step in range(2):
+        for lower in (True, False):
+
+            @pl.when(core == (0 if lower == (step == 0) else 1))
+            def _(lower=lower):
+                received = from_below if lower else from_above
+                outer = jnp.logical_not(has_down if lower else has_up)
+                for side in range(2):
+                    when(has_down if lower else has_up, row_copies[0 if lower else 1, side].wait_recv)
+                    at = cols[side]
+                    add = jnp.where(outer, 0.0, received[:, :, at])
+                    side_out[side, 1 if lower else 0] = grid[:, pl.ds(cells if lower else margin, margin), at] + add
+
+        h = 1 - core if step == 0 else core
+        for side, peer in ((0, west), (1, east)):
+            copy = remote(
+                side_out.at[side, h], from_side.at[side, h], out_send.at[side, step], out_recv.at[side, step], ty, peer
+            )
+            when(has_side[side], copy.start)
+            side_copies.append((side, copy))
+        if step == 0:
+            to_line(0)
+    for c in range(1, chunks):
+        to_line(c)
 
     backs, pairs = [], []
     for c in range(chunks):
@@ -531,10 +542,9 @@
 
 
 def shards(object_field, probe_modes, intensities, offsets, counts):
-    chunks = 2
     cells = object_field.shape[1]
     margin, size = cells // 2, 2 * cells
-    modes = probe_modes.shape[1]
+    modes = chunks = probe_modes.shape[1]
     cap = intensities.shape[2]
     rows = 2 * modes * cells
     plane, line = lax.axis_size("ty"), lax.axis_size("tx") // 2
@@ -546,7 +556,7 @@
     vmem = pltpu.VMEM
     anywhere = pl.BlockSpec(memory_space=pltpu.HBM)
     inner, total = pl.pallas_call(
-        functools.partial(kernel, chunks),
+        kernel,
         out_shape=(jax.ShapeDtypeStruct((2, cells, cells), F32), jax.ShapeDtypeStruct((rows, cells), F32)),
         in_specs=[anywhere] * 9,
         out_specs=(VMEM, VMEM),
@@ -558,7 +568,7 @@
             vmem(backward.shape, BF16),
             vmem(order.shape, BF16),
             vmem(order.shape, BF16),
-            vmem((2, margin, cells), F32),
+            vmem((cap, 2, margin, cells), F32),
             vmem((cap, 2, 3 * cells // 8, 8, size), F32),
             vmem((rows, cells), F32),
             vmem((2, size, size), F32),
@@ -570,8 +580,10 @@
             vmem((chunks, plane, piece, cells), F32),
             vmem((chunks, line, piece, cells), F32),
             vmem((cap, 2, cells, cells), F32),
+            vmem((cap, 2, cells, cells), F32),
+            vmem((cap, modes, 2, cells, cells), F32),
             pltpu.SMEM((plane, 2 * line), jnp.int32),
-            pltpu.SMEM((1, 1, cap, 2), jnp.int32),
+            pltpu.SMEM((1, 1, 2, cap), jnp.int32),
             dma((9,)),
             dma((2, 2)), dma((2, 2)), dma((2, 3)), dma((2, 3)),
             dma((2, 3)), dma((2, 3)), dma((2, 2)), dma((2, 2)),
@@ -579,13 +591,25 @@
             dma((chunks, plane)), dma((chunks, plane)), dma((chunks, line)), dma((chunks, line)),
             dma((chunks, plane)), dma((chunks, plane)), dma((chunks, plane)), dma((chunks, plane)),
         ],
-        compiler_params=pltpu.CompilerParams(collective_id=0, has_side_effects=True),
+        compiler_params=pltpu.CompilerParams(collective_id=0, has_side_effects=True, vmem_limit_bytes=44 * 2**20),
         name="gradient",
     )(
-        counts, offsets, object_field.reshape(2, cells // 8, 8, cells), probe_modes, intensities,
-        jnp.asarray(forward), jnp.asarray(backward), jnp.asarray(order), jnp.asarray(order.T),
-    )
-    return inner, total.reshape(probe_modes.shape)
+        *[
+            pltpu.with_memory_space_constraint(x, pltpu.HBM)
+            for x in (
+                counts,
+                offsets.swapaxes(2, 3),
+                object_field.reshape(2, cells // 8, 8, cells),
+                probe_modes,
+                intensities,
+                jnp.asarray(forward),
+                jnp.asarray(backward),
+                jnp.asarray(order),
+                jnp.asarray(order.T),
+            )
+        ]
+    )
+    return inner, total.reshape(modes, 2, cells, cells).swapaxes(0, 1)
 
 
 def solution(mesh):

time: 80.6 us -> 76.7 us (0.952)
  local copies, waits for them, and re-layouts: 4.27 us -> 1.83 us
  Pallas kernels: 75.6 us -> 74.2 us
    unnamed x7 -> x1, local copies, waits for them, and re-layouts: 4.27 us -> 0.79 us
    pallas_call x1, Pallas kernels: 75.6 us -> 74.2 us  [shards(): pl.pallas_call(kernel, out_shape=(jax.ShapeDtypeStruct((2, cells, cells),...]
    reshape x0 -> x1, local copies, waits for them, and re-layouts: none -> 1.04 us  [shards(): return (inner, total.reshape(modes, 2, cells, cells).swapaxes(0, 1))]
where the time goes in v4:
time: 76.7 us
  Pallas kernels  74.2 us (97%)
  local copies, waits for them, and re-layouts  1.83 us (2%)
    pallas_call x1, Pallas kernels, shards(): pl.pallas_call(kernel, out_shape=(jax.ShapeDtypeStruct((2, cells, cells),...  74.2 us

profile of v4, /device:TPU:1, one launch (start us, length us, event | category | flops | bytes accessed | tf_op | source)
XLA Modules:
  0.0 76.7 jit_solution(13796731400592714224)
XLA Ops:
  0.6 74.2 %gradient.1 = (f32[2,256,256]{2,1,0:T(8,128)S(1)}, f32[1024,256]{1,0:T(8,128)S(1)}) custom-call(s32[16,16]{1,0:T(8,128)} %counts_any.1, s32[1,1,2,3]{3,2,1,0:T(2,128)} %bitcast.9, f32[2,32,8,256]{3,2,1,0:T(8,128)} %bitcast.8, f32[2,2,256,256]{3,2,1,0:T(8,128)} %probe_any.1, f32[1,1,3,256,256]{4,3,2,1,0:T(8,128)} %measured_any.1, ...), custom_call_target="tpu_custom_call" | custom-call | tf_op jit(solution)/shard_map/gradient/pallas_call | solution.py:558
  74.8 1.0 %copy.13 = f32[2,2,256,256]{3,2,0,1:T(8,128)} copy(f32[2,2,256,256]{3,2,1,0:T(8,128)S(1)} %bitcast.6) | data formatting | bytes 2097152 | tf_op jit(solution)/shard_map/reshape | solution.py:612
  75.9 0.8 %copy.15 = f32[2,256,256]{2,1,0:T(8,128)} copy(f32[2,256,256]{2,1,0:T(8,128)S(1)} %get-tuple-element.8) | data formatting | bytes 1048576

commit v5 on v4

--- a/solution.py
+++ b/solution.py
@@ -466,7 +466,8 @@
         line_copies.append(copies)
 
     side_copies = []
-    for step in range(2):
+
+    def to_sides(step):
         for lower in (True, False):
 
             @pl.when(core == (0 if lower == (step == 0) else 1))
@@ -486,10 +487,11 @@
             )
             when(has_side[side], copy.start)
             side_copies.append((side, copy))
-        if step == 0:
-            to_line(0)
-    for c in range(1, chunks):
-        to_line(c)
+
+    to_sides(0)
+    to_line(0)
+    to_line(1)
+    to_sides(1)
 
     backs, pairs = [], []
     for c in range(chunks):

time: 76.7 us -> 73.4 us (0.957)
  Pallas kernels: 74.2 us -> 70.8 us
    pallas_call x1, Pallas kernels: 74.2 us -> 70.8 us  [shards(): pl.pallas_call(kernel, out_shape=(jax.ShapeDtypeStruct((2, cells, cells),...]
where the time goes in v5:
time: 73.4 us; the launch traced here: 73.3 us
  Pallas kernels  70.8 us (96%)
  local copies, waits for them, and re-layouts  1.83 us (2%)
    pallas_call x1, Pallas kernels, shards(): pl.pallas_call(kernel, out_shape=(jax.ShapeDtypeStruct((2, cells, cells),...  70.8 us

profile of v5, /device:TPU:1, one launch (start us, length us, event | category | flops | bytes accessed | tf_op | source)
XLA Modules:
  0.0 73.3 jit_solution(1635093532077366019)
XLA Ops:
  0.6 70.8 %gradient.1 = (f32[2,256,256]{2,1,0:T(8,128)S(1)}, f32[1024,256]{1,0:T(8,128)S(1)}) custom-call(s32[16,16]{1,0:T(8,128)} %counts_any.1, s32[1,1,2,3]{3,2,1,0:T(2,128)} %bitcast.9, f32[2,32,8,256]{3,2,1,0:T(8,128)} %bitcast.8, f32[2,2,256,256]{3,2,1,0:T(8,128)} %probe_any.1, f32[1,1,3,256,256]{4,3,2,1,0:T(8,128)} %measured_any.1, ...), custom_call_target="tpu_custom_call" | custom-call | tf_op jit(solution)/shard_map/gradient/pallas_call | solution.py:560
  71.4 1.0 %copy.13 = f32[2,2,256,256]{3,2,0,1:T(8,128)} copy(f32[2,2,256,256]{3,2,1,0:T(8,128)S(1)} %bitcast.6) | data formatting | bytes 2097152 | tf_op jit(solution)/shard_map/reshape | solution.py:614
  72.5 0.8 %copy.15 = f32[2,256,256]{2,1,0:T(8,128)} copy(f32[2,256,256]{2,1,0:T(8,128)S(1)} %get-tuple-element.8) | data formatting | bytes 1048576

commit v6 on v5

--- a/solution.py
+++ b/solution.py
@@ -245,6 +245,7 @@
         load.start()
 
     peers = [(up, tx), (down, tx), (ty, west), (ty, east), (mate, tx)]
+    peers += [(up, west), (up, east), (down, west), (down, east)]
     for d in range(1, plane_size):
         peers.append(plane_peer(d)[1:])
     for d in range(1, line_size):
@@ -252,6 +253,27 @@
     barrier = pltpu.get_barrier_semaphore()
     for peer in peers:
         pl.semaphore_signal(barrier, inc=1, device_id=peer, device_id_type=MESH)
+    placed[...] = jnp.zeros(placed.shape, F32)
+    part[...] = jnp.zeros(part.shape, F32)
+    ext[:, pl.ds(size // 8, 1)] = jnp.zeros((2, 1, 8, size), F32)
+    for there, rows, cols in (
+        (has_up, pl.ds(0, edge), pl.ds(0, size)),
+        (has_down, pl.ds(3 * edge, edge), pl.ds(0, size)),
+        (has_west, pl.ds(0, size // 8), pl.ds(0, margin)),
+        (has_east, pl.ds(0, size // 8), pl.ds(far, margin)),
+    ):
+
+        @pl.when(jnp.logical_not(there))
+        def _(rows=rows, cols=cols):
+            ext[:, rows, :, cols] = jnp.zeros((2, rows.size, 8, cols.size), F32)
+
+    for load in loads[:3]:
+        load.wait()
+
+    @pl.loop(0, cap)
+    def _(slot):
+        root[slot] = reordered_root(root[slot], order, order_t)
+
     pl.semaphore_wait(barrier, len(peers))
 
     sides = {}
@@ -281,28 +303,24 @@
     when(has_up, to_up.start)
     when(has_down, to_down.start)
 
-    placed[...] = jnp.zeros(placed.shape, F32)
-    part[...] = jnp.zeros(part.shape, F32)
-    ext[:, pl.ds(size // 8, 1)] = jnp.zeros((2, 1, 8, size), F32)
-    for there, rows, cols in (
-        (has_up, pl.ds(0, edge), pl.ds(0, size)),
-        (has_down, pl.ds(3 * edge, edge), pl.ds(0, size)),
-        (has_west, pl.ds(0, size // 8), pl.ds(0, margin)),
-        (has_east, pl.ds(0, size // 8), pl.ds(far, margin)),
-    ):
-
-        @pl.when(jnp.logical_not(there))
-        def _(rows=rows, cols=cols):
-            ext[:, rows, :, cols] = jnp.zeros((2, rows.size, 8, cols.size), F32)
-
-    for load in loads[:3]:
-        load.wait()
-
-    @pl.loop(0, cap)
-    def _(slot):
-        root[slot] = reordered_root(root[slot], order, order_t)
-
+    has_side, has_row = (has_west, has_east), (has_up, has_down)
+    across = (lax.rem(ty, n // 2) == 0, lax.rem(ty, n // 2) == n // 2 - 1)
     strips = (pl.ds(0, margin), pl.ds(far, margin))
+
+    def straight(direction, side):
+        src, dst, row = (0, 3 * edge, up) if direction == 0 else (edge, 0, down)
+        return remote(
+            tile.at[:, pl.ds(src, edge), :, pl.ds(margin if side == 0 else 0, margin)],
+            ext.at[:, pl.ds(dst, edge), :, strips[side]],
+            rows_send.at[direction, 1 + side],
+            rows_recv.at[direction, 1 + side],
+            row,
+            east if side == 0 else west,
+        )
+
+    for direction in range(2):
+        for side in range(2):
+            when(across[direction] & has_row[direction] & has_side[1 - side], straight(direction, side).start)
 
     def corner(direction, side):
         src, dst, peer = (edge, 3 * edge, up) if direction == 0 else (2 * edge, 0, down)
@@ -315,13 +333,13 @@
             tx,
         )
 
-    has_side, has_row = (has_west, has_east), (has_up, has_down)
     for step in range(2):
         for side in range(2):
             when(has_side[side], sides[step, side].wait_recv)
             for direction in range(2):
                 turn_now = core == (direction if step == 0 else 1 - direction)
-                when(turn_now & has_side[side] & has_row[direction], corner(direction, side).start)
+                near = jnp.logical_not(across[direction])
+                when(turn_now & near & has_side[side] & has_row[direction], corner(direction, side).start)
 
     for load in loads[3:]:
         load.wait()
@@ -331,7 +349,9 @@
         when(has_row[direction], copy.wait_send)
         when(has_row[1 - direction], copy.wait_recv)
         for side in range(2):
-            when(has_row[direction] & has_side[side], corner(direction, side).wait_send)
+            near = jnp.logical_not(across[direction])
+            when(near & has_row[direction] & has_side[side], corner(direction, side).wait_send)
+            when(across[direction] & has_row[direction] & has_side[1 - side], straight(direction, side).wait_send)
             when(has_row[1 - direction] & has_side[side], corner(direction, side).wait_recv)
 
     half = margin
@@ -442,7 +462,8 @@
             copy = remote(
                 grid.at[:, src, at], dst.at[:, :, at], down_send.at[direction, i], down_recv.at[direction, i], peer, tx
             )
-            when(has_row[direction], copy.start)
+            if i < 2:
+                when(has_row[direction], copy.start)
             row_copies[direction, i] = copy
 
     assemble(margin, cells)
@@ -491,6 +512,8 @@
     to_sides(0)
     to_line(0)
     to_line(1)
+    for direction in range(2):
+        when(has_row[direction], row_copies[direction, 2].start)
     to_sides(1)
 
     backs, pairs = [], []

time: 73.4 us -> 70.9 us (0.966)
  the two profiles are of different devices: /device:TPU:1 before, /device:TPU:39 now
where the time goes in v6:
time: 70.9 us; the launch traced here: 70.8 us
  Pallas kernels  68.3 us (96%)
  local copies, waits for them, and re-layouts  1.83 us (3%)
    pallas_call x1, Pallas kernels, shards(): pl.pallas_call(kernel, out_shape=(jax.ShapeDtypeStruct((2, cells, cells),...  68.3 us

profile of v6, /device:TPU:39, one launch (start us, length us, event | category | flops | bytes accessed | tf_op | source)
XLA Modules:
  0.0 70.8 jit_solution(9133273159082767335)
XLA Ops:
  0.6 68.3 %gradient.1 = (f32[2,256,256]{2,1,0:T(8,128)S(1)}, f32[1024,256]{1,0:T(8,128)S(1)}) custom-call(s32[16,16]{1,0:T(8,128)} %counts_any.1, s32[1,1,2,3]{3,2,1,0:T(2,128)} %bitcast.9, f32[2,32,8,256]{3,2,1,0:T(8,128)} %bitcast.8, f32[2,2,256,256]{3,2,1,0:T(8,128)} %probe_any.1, f32[1,1,3,256,256]{4,3,2,1,0:T(8,128)} %measured_any.1, ...), custom_call_target="tpu_custom_call" | custom-call | tf_op jit(solution)/shard_map/gradient/pallas_call | solution.py:583
  68.9 1.0 %copy.13 = f32[2,2,256,256]{3,2,0,1:T(8,128)} copy(f32[2,2,256,256]{3,2,1,0:T(8,128)S(1)} %bitcast.6) | data formatting | bytes 2097152 | tf_op jit(solution)/shard_map/reshape | solution.py:637
  70.0 0.8 %copy.15 = f32[2,256,256]{2,1,0:T(8,128)} copy(f32[2,256,256]{2,1,0:T(8,128)S(1)} %get-tuple-element.8) | data formatting | bytes 1048576

commit v7 on v6

--- a/solution.py
+++ b/solution.py
@@ -453,7 +453,7 @@
     assemble(far, margin)
     to_plane(chunks - 1)
 
-    row_copies = {}
+    row_copies, across_copies = {}, {}
     cols = (strips[0], strips[1], middle)
     for i, at in enumerate(cols):
         for direction, (src, dst, peer) in enumerate(
@@ -462,9 +462,19 @@
             copy = remote(
                 grid.at[:, src, at], dst.at[:, :, at], down_send.at[direction, i], down_recv.at[direction, i], peer, tx
             )
+            row_copies[direction, i] = copy
             if i < 2:
-                when(has_row[direction], copy.start)
-            row_copies[direction, i] = copy
+                over = remote(
+                    grid.at[:, src, at],
+                    dst.at[:, :, at],
+                    down_send.at[direction, i],
+                    down_recv.at[direction, i],
+                    peer,
+                    east if i else west,
+                )
+                across_copies[direction, i] = over
+                when(jnp.logical_not(across[direction]) & has_row[direction], copy.start)
+                when(across[direction] & has_row[direction] & has_side[i], over.start)
 
     assemble(margin, cells)
 
@@ -494,12 +504,15 @@
             @pl.when(core == (0 if lower == (step == 0) else 1))
             def _(lower=lower):
                 received = from_below if lower else from_above
-                outer = jnp.logical_not(has_down if lower else has_up)
+                inner_row = (has_down if lower else has_up) & jnp.logical_not(across[1 if lower else 0])
                 for side in range(2):
-                    when(has_down if lower else has_up, row_copies[0 if lower else 1, side].wait_recv)
-                    at = cols[side]
-                    add = jnp.where(outer, 0.0, received[:, :, at])
-                    side_out[side, 1 if lower else 0] = grid[:, pl.ds(cells if lower else margin, margin), at] + add
+                    at, half_row = cols[side], 1 if lower else 0
+                    side_out[side, half_row] = grid[:, pl.ds(cells if lower else margin, margin), at]
+
+                    @pl.when(inner_row)
+                    def _(side=side, at=at, half_row=half_row):
+                        row_copies[1 - half_row, side].wait_recv()
+                        side_out[side, half_row] = side_out[side, half_row] + received[:, :, at]
 
         h = 1 - core if step == 0 else core
         for side, peer in ((0, west), (1, east)):
@@ -538,6 +551,9 @@
 
     for direction in range(2):
         when(has_row[1 - direction], row_copies[direction, 2].wait_recv)
+        for i in range(2):
+            there = across[1 - direction] & has_row[1 - direction] & has_side[1 - i]
+            when(there, across_copies[direction, i].wait_recv)
     for side, copy in side_copies:
         when(has_side[side], copy.wait_send)
         when(has_side[1 - side], copy.wait_recv)
@@ -547,9 +563,16 @@
         value = grid[:, pl.ds((h + 1) * margin, margin), middle] + jnp.where(outer, 0.0, received[:, :, middle])
         from_west = jnp.where(has_west, from_side[1, h], 0.0)
         from_east = jnp.where(has_east, from_side[0, h], 0.0)
+        over = across[h] & has_row[h]
+        from_west = from_west + jnp.where(over & has_west, received[:, :, strips[1]], 0.0)
+        from_east = from_east + jnp.where(over & has_east, received[:, :, strips[0]], 0.0)
         inner[:, pl.ds(h * margin, margin), :] = value + jnp.concatenate([from_west, from_east], 2)
-    for (direction, _), copy in row_copies.items():
-        when(has_row[direction], copy.wait_send)
+    for (direction, i), copy in row_copies.items():
+        if i == 2:
+            when(has_row[direction], copy.wait_send)
+        else:
+            when(jnp.logical_not(across[direction]) & has_row[direction], copy.wait_send)
+            when(across[direction] & has_row[direction] & has_side[i], across_copies[direction, i].wait_send)
 
     for c in range(chunks):
         for d in range(1, plane_size):

time: 70.9 us -> 68.5 us (0.966)
  the two profiles are of different devices: /device:TPU:39 before, /device:TPU:1 now
where the time goes in v7:
time: 68.5 us; the launch traced here: 68 us
  Pallas kernels  65.6 us (96%)
  local copies, waits for them, and re-layouts  1.83 us (3%)
    pallas_call x1, Pallas kernels, shards(): pl.pallas_call(kernel, out_shape=(jax.ShapeDtypeStruct((2, cells, cells),...  65.6 us

profile of v7, /device:TPU:1, one launch (start us, length us, event | category | flops | bytes accessed | tf_op | source)
XLA Modules:
  0.0 68.0 jit_solution(16918247537000753895)
XLA Ops:
  0.6 65.6 %gradient.1 = (f32[2,256,256]{2,1,0:T(8,128)S(1)}, f32[1024,256]{1,0:T(8,128)S(1)}) custom-call(s32[16,16]{1,0:T(8,128)} %counts_any.1, s32[1,1,2,3]{3,2,1,0:T(2,128)} %bitcast.9, f32[2,32,8,256]{3,2,1,0:T(8,128)} %bitcast.8, f32[2,2,256,256]{3,2,1,0:T(8,128)} %probe_any.1, f32[1,1,3,256,256]{4,3,2,1,0:T(8,128)} %measured_any.1, ...), custom_call_target="tpu_custom_call" | custom-call | tf_op jit(solution)/shard_map/gradient/pallas_call | solution.py:606
  66.2 1.0 %copy.13 = f32[2,2,256,256]{3,2,0,1:T(8,128)} copy(f32[2,2,256,256]{3,2,1,0:T(8,128)S(1)} %bitcast.6) | data formatting | bytes 2097152 | tf_op jit(solution)/shard_map/reshape | solution.py:660
  67.2 0.8 %copy.15 = f32[2,256,256]{2,1,0:T(8,128)} copy(f32[2,256,256]{2,1,0:T(8,128)S(1)} %get-tuple-element.8) | data formatting | bytes 1048576
